TPU v7x, 32 devices: a whole 2x2x4 slice. The times are simulated.
32 devices in a mesh: dp: 8 (over y, x, core), fsdp: 4 (over z).
Axes of the slice: x: 2, y: 2, z: 4, core: 2. Of those that a mesh axis runs over, the one named last changes fastest.
Arguments:
- layer_input: bfloat16 [2, 8, 1024, 1152], P(None, 'dp', 'fsdp'), may hold values from -6 to 6
- output_gradient: bfloat16 [2, 8, 1024, 1152], P(None, 'dp', 'fsdp'), may hold values from -6 to 6
- prefix_length: int32 [2, 8], P(None, 'dp'), may hold values from 0 to 1024
- attention_gain: bfloat16 [1152], P(('dp', 'fsdp')), may hold values from 0.5 to 1.5
- inward: bfloat16 [1152, 1536], P(('dp', 'fsdp')), may hold values from -0.1875 to 0.1875
- inward_down: bfloat16 [1152, 256], P(('dp', 'fsdp')), may hold values from -0.1875 to 0.1875
- inward_up: bfloat16 [256, 1536], P(('dp', 'fsdp')), may hold values from -0.1875 to 0.1875
- outward: bfloat16 [1024, 1152], P(('dp', 'fsdp')), may hold values from -1.5 to 1.5
- outward_down: bfloat16 [1024, 256], P(('dp', 'fsdp')), may hold values from -1.5 to 1.5
- outward_up: bfloat16 [256, 1152], P(('dp', 'fsdp')), may hold values from -0.1875 to 0.1875
- feedforward_gain: bfloat16 [1152], P(('dp', 'fsdp')), may hold values from 0.5 to 1.5
- widening: bfloat16 [1152, 13824], P(('dp', 'fsdp')), may hold values from -0.1875 to 0.1875
- widening_down: bfloat16 [1152, 256], P(('dp', 'fsdp')), may hold values from -0.1875 to 0.1875
- widening_up: bfloat16 [256, 13824], P(('dp', 'fsdp')), may hold values from -0.1875 to 0.1875
- narrowing: bfloat16 [6912, 1152], P(('dp', 'fsdp')), may hold values from -0.078125 to 0.078125
- narrowing_down: bfloat16 [6912, 256], P(('dp', 'fsdp')), may hold values from -0.078125 to 0.078125
- narrowing_up: bfloat16 [256, 1152], P(('dp', 'fsdp')), may hold values from -0.1875 to 0.1875
Outputs:
- layer_output: bfloat16 [2, 8, 1024, 1152], P(None, 'dp', 'fsdp')
- input_gradient: float32 [2, 8, 1024, 1152], P(None, 'dp', 'fsdp')
- attention_gain_gradient: float32 [1152], P(('dp', 'fsdp'))
- inward_gradient: float32 [1152, 1536], P(('dp', 'fsdp'))
- inward_down_gradient: float32 [1152, 256], P(('dp', 'fsdp'))
- inward_up_gradient: float32 [256, 1536], P(('dp', 'fsdp'))
- outward_gradient: float32 [1024, 1152], P(('dp', 'fsdp'))
- outward_down_gradient: float32 [1024, 256], P(('dp', 'fsdp'))
- outward_up_gradient: float32 [256, 1152], P(('dp', 'fsdp'))
- feedforward_gain_gradient: float32 [1152], P(('dp', 'fsdp'))
- widening_gradient: float32 [1152, 13824], P(('dp', 'fsdp'))
- widening_down_gradient: float32 [1152, 256], P(('dp', 'fsdp'))
- widening_up_gradient: float32 [256, 13824], P(('dp', 'fsdp'))
- narrowing_gradient: float32 [6912, 1152], P(('dp', 'fsdp'))
- narrowing_down_gradient: float32 [6912, 256], P(('dp', 'fsdp'))
- narrowing_up_gradient: float32 [256, 1152], P(('dp', 'fsdp'))
All inputs are finite; a program needn't handle non-finite values.
Results may differ from a plain program's by a relative error of at most 0.019.
Values may be sent and summed in bfloat16 or wider, within the bound.
A program may use at most 448 MiB of HBM per device.

v0:
```python
import jax
import jax.numpy as jnp
from jax import lax
from jax.sharding import PartitionSpec as P

FF = 6912
HEADS = 4
HDIM = 256


EPSILON = 1e-06
THETA = 10000.0
LANES = 128


def shortened(shard):
    return jax.tree.map(lambda a: a.astype(jnp.bfloat16) if a.dtype == jnp.float32 else a, shard)


def rms_scale(row_block, gain):
    factor = lax.rsqrt(jnp.mean(row_block * row_block, axis=-1, keepdims=True) + EPSILON)
    return row_block * factor * gain


def product(left, right):
    return jnp.dot(left, right, preferred_element_type=jnp.float32)


def contract_rows(left, right):
    return lax.dot_general(
        left, right, (((0,), (0,)), ((), ())), preferred_element_type=jnp.float32
    )


def against(left, right):
    return lax.dot_general(
        left, right, (((1,), (1,)), ((), ())), preferred_element_type=jnp.float32
    )


def adapted(row_block, base, reducer, expander):
    inner_rows = product(row_block, reducer).astype(jnp.bfloat16)
    return (product(row_block, base) + product(inner_rows, expander), inner_rows)


def adapted_back(row_block, inner_rows, upstream, base, reducer, expander):
    base_grad = contract_rows(row_block, upstream)
    expander_grad = contract_rows(inner_rows, upstream)
    inner_grad = against(upstream, expander).astype(jnp.bfloat16)
    reducer_grad = contract_rows(row_block, inner_grad)
    rows_grad = against(upstream, base) + against(inner_grad, reducer)
    return (rows_grad, (base_grad, reducer_grad, expander_grad))


def rotation(positions, width):
    halfway = width // 2
    frequency = jnp.power(THETA, -2.0 * jnp.arange(halfway, dtype=jnp.float32) / width)
    angles = positions.astype(jnp.float32)[:, None] * frequency[None, :]
    return (jnp.cos(angles), jnp.sin(angles))


def rotate(values, cosine, sine_part):
    halfway = values.shape[-1] // 2
    leading = values[..., :halfway]
    second = values[..., halfway:]
    return jnp.concatenate(
        [leading * cosine - second * sine_part, second * cosine + leading * sine_part], axis=-1
    )


def gated(gate_part, upper_part):
    return jax.nn.gelu(gate_part, approximate=True) * upper_part


def flatten_all(arrays):
    return tuple((item if item.ndim == 1 else item.reshape(-1, LANES) for item in arrays))


def restore_all(arrays, columns):
    return tuple(
        (item if width == 0 else item.reshape(-1, width) for item, width in zip(arrays, columns))
    )


def widths_of(arrays):
    return tuple((0 if item.ndim == 1 else item.shape[1] for item in arrays))


def fetch_attention(params):
    gathered = lax.all_gather(shortened(flatten_all(params)), ("dp", "fsdp"), axis=0, tiled=True)
    return restore_all(gathered, widths_of(params))


def fetch_feed(params):
    gathered = lax.all_gather(shortened(flatten_all(params)), ("dp", "fsdp"), axis=0, tiled=True)
    return restore_all(gathered, widths_of(params))


def sum_at_end(gradients):
    summed = lax.psum_scatter(
        flatten_all(gradients), ("dp", "fsdp"), scatter_dimension=0, tiled=True
    )
    return restore_all(summed, widths_of(gradients))


def per_device(
    layer_input,
    output_gradient,
    prefix_length,
    attention_gain,
    inward,
    inward_down,
    inward_up,
    outward,
    outward_down,
    outward_up,
    feedforward_gain,
    widening,
    widening_down,
    widening_up,
    narrowing,
    narrowing_down,
    narrowing_up,
):
    attention_local = (
        attention_gain,
        inward,
        inward_down,
        inward_up,
        outward,
        outward_down,
        outward_up,
    )
    feed_local = (
        feedforward_gain,
        widening,
        widening_down,
        widening_up,
        narrowing,
        narrowing_down,
        narrowing_up,
    )
    micro_count = layer_input.shape[0]
    row_count = layer_input.shape[2]
    query_width = HEADS * HDIM
    scale = HDIM ** (-0.5)
    positions = lax.axis_index("fsdp") * row_count + jnp.arange(row_count, dtype=jnp.int32)
    cosine, sine_part = rotation(positions, HDIM)
    head_cosine = cosine[:, None, :]
    head_sine = sine_part[:, None, :]
    outputs = []
    input_grads = []
    totals = None
    for batch_index in range(micro_count):
        attention_full = fetch_attention(attention_local)
        (
            first_gain,
            inward_full,
            inward_down_full,
            inward_up_full,
            outward_full,
            outward_down_full,
            outward_up_full,
        ) = attention_full
        first_gain = first_gain.astype(jnp.float32)
        residual = layer_input[batch_index, 0].astype(jnp.float32)
        normed_first = rms_scale(residual, first_gain).astype(jnp.bfloat16)
        joint, joint_inner = adapted(normed_first, inward_full, inward_down_full, inward_up_full)
        queries = rotate(
            joint[:, :query_width].reshape(row_count, HEADS, HDIM), head_cosine, head_sine
        ).astype(jnp.bfloat16)
        own_keys = rotate(joint[:, query_width : query_width + HDIM], cosine, sine_part).astype(
            jnp.bfloat16
        )
        own_values = joint[:, query_width + HDIM :].astype(jnp.bfloat16)
        all_keys, all_values = (
            lax.all_gather(own_keys, "fsdp", axis=0, tiled=True),
            lax.all_gather(own_values, "fsdp", axis=0, tiled=True),
        )
        key_pos = jnp.arange(all_keys.shape[0], dtype=jnp.int32)
        limit = prefix_length[batch_index, 0]
        visible = (key_pos[None, :] <= positions[:, None]) | (key_pos[None, :] < limit)

        def masked_scores():
            raw_scores = (
                jnp.einsum("rhd,kd->hrk", queries, all_keys, preferred_element_type=jnp.float32)
                * scale
            )
            return jnp.where(visible[None], raw_scores, -1e30)

        scores = masked_scores()
        peak = jnp.max(scores, axis=-1, keepdims=True)
        logsum = peak + jnp.log(jnp.sum(jnp.exp(scores - peak), axis=-1, keepdims=True))
        probs_low = jnp.exp(scores - logsum).astype(jnp.bfloat16)
        mixed = jnp.einsum("hrk,kd->rhd", probs_low, all_values, preferred_element_type=jnp.float32)
        mixed = mixed.reshape(row_count, query_width).astype(jnp.bfloat16)
        branch, mixed_inner = adapted(mixed, outward_full, outward_down_full, outward_up_full)
        middle = residual + branch
        feed_full = fetch_feed(feed_local)
        (
            second_gain,
            widening_full,
            widening_down_full,
            widening_up_full,
            narrowing_full,
            narrowing_down_full,
            narrowing_up_full,
        ) = feed_full
        second_gain = second_gain.astype(jnp.float32)
        normed_second = rms_scale(middle, second_gain).astype(jnp.bfloat16)
        spread, spread_inner = adapted(
            normed_second, widening_full, widening_down_full, widening_up_full
        )
        activated, gated_back = jax.vjp(gated, spread[:, :FF], spread[:, FF:])
        activated = activated.astype(jnp.bfloat16)
        shrink, shrink_inner = adapted(
            activated, narrowing_full, narrowing_down_full, narrowing_up_full
        )
        outputs.append((middle + shrink).astype(jnp.bfloat16))
        upstream = output_gradient[batch_index, 0]
        feed_back_full = fetch_feed(feed_local)
        (
            second_gain_back,
            widening_back,
            widening_down_back,
            widening_up_back,
            narrowing_back,
            narrowing_down_back,
            narrowing_up_back,
        ) = feed_back_full
        act_grad, narrowing_grads = adapted_back(
            activated,
            shrink_inner,
            upstream,
            narrowing_back,
            narrowing_down_back,
            narrowing_up_back,
        )
        gate_grad, upper_grad = gated_back(act_grad)
        spread_grad = jnp.concatenate([gate_grad, upper_grad], axis=1).astype(jnp.bfloat16)
        second_rows_grad, widening_grads = adapted_back(
            normed_second,
            spread_inner,
            spread_grad,
            widening_back,
            widening_down_back,
            widening_up_back,
        )
        second_norm_back = jax.vjp(rms_scale, middle, second_gain_back.astype(jnp.float32))[1]
        middle_back, second_gain_grad = second_norm_back(second_rows_grad)
        middle_grad = upstream.astype(jnp.float32) + middle_back
        attention_back_full = fetch_attention(attention_local)
        (
            first_gain_back,
            inward_back,
            inward_down_back,
            inward_up_back,
            outward_back,
            outward_down_back,
            outward_up_back,
        ) = attention_back_full
        branch_grad = middle_grad.astype(jnp.bfloat16)
        mixed_grad, outward_grads = adapted_back(
            mixed, mixed_inner, branch_grad, outward_back, outward_down_back, outward_up_back
        )
        mixed_grad = mixed_grad.astype(jnp.bfloat16).reshape(row_count, HEADS, HDIM)
        probs_again = jnp.exp(masked_scores() - logsum)
        prob_grad = jnp.einsum(
            "rhd,kd->hrk", mixed_grad, all_values, preferred_element_type=jnp.float32
        )
        center = jnp.sum(probs_again * prob_grad, axis=-1, keepdims=True)
        score_grad = (probs_again * (prob_grad - center)).astype(jnp.bfloat16)
        query_grad = (
            jnp.einsum("hrk,kd->rhd", score_grad, all_keys, preferred_element_type=jnp.float32)
            * scale
        )
        key_grad = (
            jnp.einsum("hrk,rhd->kd", score_grad, queries, preferred_element_type=jnp.float32)
            * scale
        )
        value_grad = jnp.einsum(
            "hrk,rhd->kd",
            probs_again.astype(jnp.bfloat16),
            mixed_grad,
            preferred_element_type=jnp.float32,
        )
        own_key_grad, own_value_grad = (
            lax.psum_scatter(
                key_grad.astype(jnp.bfloat16), "fsdp", scatter_dimension=0, tiled=True
            ).astype(jnp.float32),
            lax.psum_scatter(
                value_grad.astype(jnp.bfloat16), "fsdp", scatter_dimension=0, tiled=True
            ).astype(jnp.float32),
        )
        joint_grad = jnp.concatenate(
            [
                rotate(query_grad, head_cosine, -head_sine).reshape(row_count, query_width),
                rotate(own_key_grad, cosine, -sine_part),
                own_value_grad,
            ],
            axis=1,
        ).astype(jnp.bfloat16)
        first_rows_grad, inward_grads = adapted_back(
            normed_first, joint_inner, joint_grad, inward_back, inward_down_back, inward_up_back
        )
        first_norm_back = jax.vjp(rms_scale, residual, first_gain_back.astype(jnp.float32))[1]
        residual_back, first_gain_grad = first_norm_back(first_rows_grad)
        input_grads.append(middle_grad + residual_back)
        gradients = (
            (first_gain_grad,)
            + inward_grads
            + outward_grads
            + (second_gain_grad,)
            + widening_grads
            + narrowing_grads
        )
        totals = (
            gradients
            if totals is None
            else tuple((total + grad_part for total, grad_part in zip(totals, gradients)))
        )
    totals = sum_at_end(totals)
    layer_output = jnp.stack(outputs)[:, None]
    input_gradient = jnp.stack(input_grads)[:, None]
    return (layer_output, input_gradient) + tuple(totals)


def solution(mesh):
    in_specs = (
        P(None, "dp", "fsdp", None),
        P(None, "dp", "fsdp", None),
        P(None, "dp"),
        P(("dp", "fsdp")),
        P(("dp", "fsdp"), None),
        P(("dp", "fsdp"), None),
        P(("dp", "fsdp"), None),
        P(("dp", "fsdp"), None),
        P(("dp", "fsdp"), None),
        P(("dp", "fsdp"), None),
        P(("dp", "fsdp")),
        P(("dp", "fsdp"), None),
        P(("dp", "fsdp"), None),
        P(("dp", "fsdp"), None),
        P(("dp", "fsdp"), None),
        P(("dp", "fsdp"), None),
        P(("dp", "fsdp"), None),
    )
    out_specs = (
        P(None, "dp", "fsdp", None),
        P(None, "dp", "fsdp", None),
        P(("dp", "fsdp")),
        P(("dp", "fsdp"), None),
        P(("dp", "fsdp"), None),
        P(("dp", "fsdp"), None),
        P(("dp", "fsdp"), None),
        P(("dp", "fsdp"), None),
        P(("dp", "fsdp"), None),
        P(("dp", "fsdp")),
        P(("dp", "fsdp"), None),
        P(("dp", "fsdp"), None),
        P(("dp", "fsdp"), None),
        P(("dp", "fsdp"), None),
        P(("dp", "fsdp"), None),
        P(("dp", "fsdp"), None),
    )
    return jax.shard_map(
        per_device, mesh=mesh, in_specs=in_specs, out_specs=out_specs, check_vma=False
    )
```

profile of v0, /device:TPU:0, one launch (start us, length us, event | category | flops | bytes accessed | tf_op | source)
XLA Modules:
  0.0 3129.8 jit_solution(15749727596502095447)
XLA Ops:
  20.2 42.6 %all-reduce.11 = (bf16[1152]{0:T(1024)(128)(2,1)S(1)}, bf16[1152]{0:T(1024)(128)(2,1)S(1)}) all-reduce(bf16[1152]{0:T(1024)(128)(2,1)S(1)} %dynamic-update-slice, bf16[1152]{0:T(1024)(128)(2,1)S(1)} %dynamic-update-slice.1), channel_id=1, replica_groups=mesh['dp'=8,'fsdp'=4] {'dp','fsdp'}, use_global_device_ids=true, to_apply=%add | all-reduce | flops 2304 | bytes 9216
  64.3 72.0 %all_gather.43 = bf16[2048,128]{1,0:T(8,128)(2,1)S(1)} all-gather(bf16[64,128]{1,0:T(8,128)(2,1)S(1)} %reshape.599), channel_id=1, replica_groups=mesh['dp'=8,'fsdp'=4] {'dp','fsdp'}, dimensions={0}, use_global_device_ids=true | all-gather | bytes 540672 | tf_op jit(solution)/shard_map/all_gather | solution.py:90
  137.3 70.8 %all_gather.51 = bf16[2304,128]{1,0:T(8,128)(2,1)S(1)} all-gather(bf16[72,128]{1,0:T(8,128)(2,1)S(1)} %reshape.613), channel_id=1, replica_groups=mesh['dp'=8,'fsdp'=4] {'dp','fsdp'}, dimensions={0}, use_global_device_ids=true | all-gather | bytes 608256 | tf_op jit(solution)/shard_map/all_gather | solution.py:95
  208.7 76.2 %all_gather.47 = bf16[2304,128]{1,0:T(8,128)(2,1)S(1)} all-gather(bf16[72,128]{1,0:T(8,128)(2,1)S(1)} %reshape.605), channel_id=1, replica_groups=mesh['dp'=8,'fsdp'=4] {'dp','fsdp'}, dimensions={0}, use_global_device_ids=true | all-gather | bytes 608256 | tf_op jit(solution)/shard_map/all_gather | solution.py:95
  285.9 78.0 %all_gather.44 = bf16[2304,128]{1,0:T(8,128)(2,1)S(1)} all-gather(bf16[72,128]{1,0:T(8,128)(2,1)S(1)} %reshape.601), channel_id=1, replica_groups=mesh['dp'=8,'fsdp'=4] {'dp','fsdp'}, dimensions={0}, use_global_device_ids=true | all-gather | bytes 608256 | tf_op jit(solution)/shard_map/all_gather | solution.py:90
  365.4 75.2 %all_gather.38 = bf16[2304,128]{1,0:T(8,128)(2,1)S(1)} all-gather(bf16[72,128]{1,0:T(8,128)(2,1)} %reshape.592), channel_id=1, replica_groups=mesh['dp'=8,'fsdp'=4] {'dp','fsdp'}, dimensions={0}, use_global_device_ids=true | all-gather | bytes 608256 | tf_op jit(solution)/shard_map/all_gather | solution.py:90
  441.7 92.0 %all_gather.39 = bf16[3072,128]{1,0:T(8,128)(2,1)} all-gather(bf16[96,128]{1,0:T(8,128)(2,1)} %reshape.594), channel_id=1, replica_groups=mesh['dp'=8,'fsdp'=4] {'dp','fsdp'}, dimensions={0}, use_global_device_ids=true | all-gather | bytes 811008 | tf_op jit(solution)/shard_map/all_gather | solution.py:90
  581.4 20.3 all_gather.52
  601.7 16.3 all_gather.40
  674.3 30.1 reshape.610
  736.4 52.1 %reshape.604 = bf16[1152,13824]{1,0:T(8,128)(2,1)} reshape(bf16[124416,128]{1,0:T(8,128)(2,1)} %all-gather.11.cloned.1.call-done) | data formatting | bytes 63700992 | tf_op jit(solution)/shard_map/reshape | solution.py:81
  788.5 18.1 fusion.187
  842.2 19.0 fusion.177
  865.1 18.0 fusion.190
  912.5 18.8 fusion.174
  1021.6 21.2 reduce-scatter.31.cloned.1.call-done
  1135.5 17.7 fusion.83
  1153.2 23.9 convolution_add_fusion.1
  1177.2 32.8 %reshape.638 = f32[62208,128]{1,0:T(8,128)} reshape(f32[6912,1152]{1,0:T(8,128)} %convolution_add_fusion.1) | data formatting | bytes 63700992 | tf_op jit(solution)/shard_map/reshape | solution.py:76
  1210.3 26.4 fusion.176
  1236.6 45.8 %convolution_add_fusion = f32[1152,13824]{1,0:T(8,128)} fusion(f32[1152,13824]{1,0:T(8,128)} %fusion.176, bf16[256,1152]{1,0:T(8,128)(2,1)} %copy-done.40, bf16[256,6912]{1,0:T(8,128)(2,1)} %get-tuple-element.83, bf16[256,6912]{1,0:T(8,128)(2,1)S(1)} %copy-done.34), kind=kOutput, calls=%fused_computation | convolution fusion | flops 8183808000 | bytes 135069696 | tf_op jit(solution)/shard_map/dot_general | solution.py:30
  1282.4 59.0 %reshape.632 = f32[124416,128]{1,0:T(8,128)} reshape(f32[1152,13824]{1,0:T(8,128)} %convolution_add_fusion) | data formatting | bytes 127401984 | tf_op jit(solution)/shard_map/reshape | solution.py:76
  1373.1 38.9 %all-reduce.10 = (f32[1152]{0:T(1024)}, f32[1152]{0:T(1024)}) all-reduce(f32[1152]{0:T(1024)} %add.305, f32[1152]{0:T(1024)} %add.312), channel_id=6, replica_groups=mesh['dp'=8,'fsdp'=4] {'dp','fsdp'}, use_global_device_ids=true, to_apply=%region_20.21.clone | all-reduce | flops 2304 | bytes 18432
  1424.3 59.7 %reduce-scatter.43.cloned.1.call-done = f32[64,128]{1,0:T(8,128)} async-done(((f32[2048,128]{1,0:T(8,128)}), f32[64,128]{1,0:T(8,128)}) %reduce-scatter.43.cloned.1.call-update) | async-done | bytes 32784 | tf_op jit(solution)/shard_map/reduce_scatter | solution.py:100
  1485.4 97.3 %reduce-scatter.49.cloned.1.call-done = f32[72,128]{1,0:T(8,128)} async-done(((f32[2304,128]{1,0:T(8,128)}), f32[72,128]{1,0:T(8,128)}) %reduce-scatter.49.cloned.1.call-update) | async-done | bytes 36880
  1584.0 100.6 %reduce-scatter.39.cloned.1.call-done = f32[96,128]{1,0:T(8,128)} async-done(((f32[3072,128]{1,0:T(8,128)}), f32[96,128]{1,0:T(8,128)}) %reduce-scatter.39.cloned.1.call-update) | async-done | bytes 49168 | tf_op jit(solution)/shard_map/reduce_scatter | solution.py:100
  1686.0 110.5 %reduce-scatter.41.cloned.1.call-done = f32[288,128]{1,0:T(8,128)} async-done(((f32[9216,128]{1,0:T(8,128)}), f32[288,128]{1,0:T(8,128)}) %reduce-scatter.41.cloned.1.call-update) | async-done | bytes 147472 | tf_op jit(solution)/shard_map/reduce_scatter | solution.py:100
  1798.1 122.5 %reduce-scatter.47.cloned.1.call-done = f32[432,128]{1,0:T(8,128)} async-done(((f32[13824,128]{1,0:T(8,128)}), f32[432,128]{1,0:T(8,128)}) %reduce-scatter.47.cloned.1.call-update) | async-done | bytes 221200 | tf_op jit(solution)/shard_map/reduce_scatter | solution.py:100
  1922.3 122.5 %reduce-scatter.37.cloned.1.call-done = f32[432,128]{1,0:T(8,128)} async-done(((f32[13824,128]{1,0:T(8,128)}), f32[432,128]{1,0:T(8,128)}) %reduce-scatter.37.cloned.1.call-update) | async-done | bytes 221200 | tf_op jit(solution)/shard_map/reduce_scatter | solution.py:100
  2046.5 166.1 %reduce-scatter.45.cloned.1.call-done = f32[864,128]{1,0:T(8,128)} async-done(((f32[27648,128]{1,0:T(8,128)}), f32[864,128]{1,0:T(8,128)}) %reduce-scatter.45.cloned.1.call-update) | async-done | bytes 442384 | tf_op jit(solution)/shard_map/reduce_scatter | solution.py:100
  2214.5 316.5 %reduce-scatter.57.cloned.1.call-done = f32[1944,128]{1,0:T(8,128)} async-done(((f32[62208,128]{1,0:T(8,128)}), f32[1944,128]{1,0:T(8,128)}) %reduce-scatter.57.cloned.1.call-update) | async-done | bytes 995344
  2533.3 586.2 %reduce-scatter.53.cloned.1.call-done = f32[3888,128]{1,0:T(8,128)} async-done(((f32[124416,128]{1,0:T(8,128)}), f32[3888,128]{1,0:T(8,128)}) %reduce-scatter.53.cloned.1.call-update) | async-done | bytes 1990672
  (606 shorter events, 465.7 us)
Async XLA Ops:
  7.3 539.3 %all-gather.9.cloned.1.call-start = ((), (), s32[]{:S(2)}) async-start(), calls=%async_computation.17 | async-start | bytes 2433024 | tf_op jit(solution)/shard_map/all_gather | solution.py:90
  9.0 542.2 %all-gather.7.cloned.1.call-start = ((), (), s32[]{:S(2)}) async-start(), calls=%async_computation.16 | async-start | bytes 3649536 | tf_op jit(solution)/shard_map/all_gather | solution.py:90
  10.8 561.9 %all-gather.17.cloned.1.call-start = ((), (), s32[]{:S(2)}) async-start(), calls=%async_computation.21 | async-start | bytes 3649536 | tf_op jit(solution)/shard_map/all_gather | solution.py:95
  12.5 648.9 %all-gather.13.cloned.1.call-start = ((), (), s32[]{:S(2)}) async-start(), calls=%async_computation.19 | async-start | bytes 7299072 | tf_op jit(solution)/shard_map/all_gather | solution.py:95
  14.5 659.8 %all-gather.15.cloned.1.call-start = ((), (), s32[]{:S(2)}) async-start(), calls=%async_computation.20 | async-start | bytes 16422912 | tf_op jit(solution)/shard_map/all_gather | solution.py:95
  17.0 719.5 %all-gather.11.cloned.1.call-start = ((), (), s32[]{:S(2)}) async-start(), calls=%async_computation.18 | async-start | bytes 32845824 | tf_op jit(solution)/shard_map/all_gather | solution.py:95
  19.6 976.2 %reduce-scatter.29.cloned.1.call-start = ((), (), s32[]{:S(2)}) async-start(), calls=%async_computation.22 | async-start | bytes 655360 | tf_op jit(solution)/shard_map/reduce_scatter | solution.py:288
  62.8 502.6 %copy-start.103 = (f32[1152]{0:T(1024)}, f32[1152]{0:T(1024)S(1)}, u32[]{:S(2)}) copy-start(f32[1152]{0:T(1024)S(1)} %convert_element_type.212) | copy-start | bytes 13828
  62.8 877.1 %copy-start.120 = (f32[1152]{0:T(1024)}, f32[1152]{0:T(1024)S(1)}, u32[]{:S(2)}) copy-start(f32[1152]{0:T(1024)S(1)} %convert_element_type.222) | copy-start | bytes 13828
  208.7 334.7 %copy-start.52 = (bf16[256,1152]{1,0:T(8,128)(2,1)}, bf16[256,1152]{1,0:T(8,128)(2,1)S(1)}, u32[]{:S(2)}) copy-start(bf16[256,1152]{1,0:T(8,128)(2,1)S(1)} %reshape.614) | copy-start | bytes 1769476
  284.9 255.2 %copy-start.10 = (bf16[2,1,256,1152]{3,2,1,0:T(8,128)(2,1)S(1)}, bf16[2,1,256,1152]{3,2,1,0:T(8,128)(2,1)}, u32[]{:S(2)}) copy-start(bf16[2,1,256,1152]{3,2,1,0:T(8,128)(2,1)} %param.17) | copy-start | bytes 3538948
  363.9 178.5 %copy-start.18 = (bf16[2,1,256,1152]{3,2,1,0:T(8,128)(2,1)S(1)}, bf16[2,1,256,1152]{3,2,1,0:T(8,128)(2,1)}, u32[]{:S(2)}) copy-start(bf16[2,1,256,1152]{3,2,1,0:T(8,128)(2,1)} %param.18) | copy-start | bytes 3538948
  551.2 107.0 %copy-start = (bf16[1024,1152]{1,0:T(8,128)(2,1)}, bf16[1024,1152]{1,0:T(8,128)(2,1)S(1)}, u32[]{:S(2)}) copy-start(bf16[1024,1152]{1,0:T(8,128)(2,1)S(1)} %reshape.598) | copy-start | bytes 7077892
  654.7 285.3 %copy-start.2 = (f32[256,1152]{1,0:T(8,128)}, f32[256,1152]{1,0:T(8,128)S(1)}, u32[]{:S(2)}) copy-start(f32[256,1152]{1,0:T(8,128)S(1)} %get-tuple-element.129) | copy-start | bytes 3538948
  654.7 285.2 %copy-start.155 = (f32[256]{0:T(256)}, f32[256]{0:T(256)S(1)}, u32[]{:S(2)}) copy-start(f32[256]{0:T(256)S(1)} %fusion.162) | copy-start | bytes 3076
  659.6 280.3 %copy-start.4 = (f32[256,1152]{1,0:T(8,128)}, f32[256,1152]{1,0:T(8,128)S(1)}, u32[]{:S(2)}) copy-start(f32[256,1152]{1,0:T(8,128)S(1)} %get-tuple-element.131) | copy-start | bytes 3538948
  660.1 279.8 %copy-start.157 = (f32[256]{0:T(256)}, f32[256]{0:T(256)S(1)}, u32[]{:S(2)}) copy-start(f32[256]{0:T(256)S(1)} %fusion.164) | copy-start | bytes 3076
  951.5 46.6 %reduce-scatter.33.cloned.1.call-start = ((), (), s32[]{:S(2)}) async-start(), calls=%async_computation.24 | async-start | bytes 655360 | tf_op jit(solution)/shard_map/reduce_scatter | solution.py:288
  960.1 60.5 %reduce-scatter.35.cloned.1.call-start = ((), (), s32[]{:S(2)}) async-start(), calls=%async_computation.25 | async-start | bytes 655360 | tf_op jit(solution)/shard_map/reduce_scatter | solution.py:291
  964.3 78.5 %reduce-scatter.31.cloned.1.call-start = ((), (), s32[]{:S(2)}) async-start(), calls=%async_computation.23 | async-start | bytes 655360 | tf_op jit(solution)/shard_map/reduce_scatter | solution.py:291
  973.5 446.6 %reduce-scatter.59.cloned.1.call-start = ((), (), s32[]{:S(2)}) async-start(), calls=%async_computation.37 | async-start | bytes 1216512
  980.4 441.1 %reduce-scatter.55.cloned.1.call-start = ((), (), s32[]{:S(2)}) async-start(), calls=%async_computation.35 | async-start | bytes 1216512
  983.4 439.5 %reduce-scatter.51.cloned.1.call-start = ((), (), s32[]{:S(2)}) async-start(), calls=%async_computation.33 | async-start | bytes 1216512
  986.4 497.5 %reduce-scatter.43.cloned.1.call-start = ((), (), s32[]{:S(2)}) async-start(), calls=%async_computation.29 | async-start | bytes 1081344 | tf_op jit(solution)/shard_map/reduce_scatter | solution.py:100
  991.9 590.8 %reduce-scatter.49.cloned.1.call-start = ((), (), s32[]{:S(2)}) async-start(), calls=%async_computation.32 | async-start | bytes 1216512
  1052.6 632.0 %reduce-scatter.39.cloned.1.call-start = ((), (), s32[]{:S(2)}) async-start(), calls=%async_computation.27 | async-start | bytes 1622016 | tf_op jit(solution)/shard_map/reduce_scatter | solution.py:100
  1059.3 737.2 %reduce-scatter.41.cloned.1.call-start = ((), (), s32[]{:S(2)}) async-start(), calls=%async_computation.28 | async-start | bytes 4866048 | tf_op jit(solution)/shard_map/reduce_scatter | solution.py:100
  1069.2 851.4 %reduce-scatter.47.cloned.1.call-start = ((), (), s32[]{:S(2)}) async-start(), calls=%async_computation.31 | async-start | bytes 7299072 | tf_op jit(solution)/shard_map/reduce_scatter | solution.py:100
  1085.9 959.0 %reduce-scatter.37.cloned.1.call-start = ((), (), s32[]{:S(2)}) async-start(), calls=%async_computation.26 | async-start | bytes 7299072 | tf_op jit(solution)/shard_map/reduce_scatter | solution.py:100
  1100.4 1112.2 %reduce-scatter.45.cloned.1.call-start = ((), (), s32[]{:S(2)}) async-start(), calls=%async_computation.30 | async-start | bytes 14598144 | tf_op jit(solution)/shard_map/reduce_scatter | solution.py:100
  1135.3 1395.6 %reduce-scatter.57.cloned.1.call-start = ((), (), s32[]{:S(2)}) async-start(), calls=%async_computation.36 | async-start | bytes 32845824
  1210.0 1909.5 %reduce-scatter.53.cloned.1.call-start = ((), (), s32[]{:S(2)}) async-start(), calls=%async_computation.34 | async-start | bytes 65691648
  (172 other events, 1668.2 us)
Sparse Core Ops, SparseCore 0:
  11.5 60.1 all-gather.8
  75.0 59.2 all-gather.6
  137.2 60.8 all-gather.16
  201.2 71.9 all-gather.12
  276.0 117.5 all-gather.14
  396.8 208.0 all-gather.10
  951.7 23.9 reduce-scatter.28
  978.0 20.1 reduce-scatter.32
  1000.4 20.1 reduce-scatter.34
  1022.7 20.0 reduce-scatter.30
  1047.9 95.3 reduce-scatter.58
  1148.2 96.0 reduce-scatter.54
  1249.4 96.1 reduce-scatter.50
  1347.7 136.2 reduce-scatter.42
  1488.9 93.6 reduce-scatter.48
  1587.7 96.8 reduce-scatter.38
  1689.9 106.5 reduce-scatter.40
  1802.1 118.5 reduce-scatter.46
  1926.3 118.5 reduce-scatter.36
  2050.7 161.8 reduce-scatter.44
  2219.0 311.8 reduce-scatter.56
  2537.3 582.0 reduce-scatter.52
where the time goes:
time: 3140 us; the launch traced here: 3130 us
  waiting for transfers between devices  1720 us (55%)
  blocking collectives  613 us (20%)
  matrix products  426 us (14%)
  local copies, waits for them, and re-layouts  330 us (11%)
    unnamed x28, waiting for transfers between devices  1000 us
    reduce_scatter x6, waiting for transfers between devices, sum_at_end(): lax.psum_scatter(flatten_all(gradients), ('dp', 'fsdp'), scatter_dimensio...  682 us
    all_gather x4, blocking collectives, fetch_attention(): lax.all_gather(shortened(flatten_all(params)), ('dp', 'fsdp'), axis=0, ti...  317 us
    dot_general x24, matrix products, contract_rows(): lax.dot_general(left, right, (((0,), (0,)), ((), ())), preferred_element_...  164 us
    reshape x24, local copies, waits for them, and re-layouts, flatten_all(): item.reshape(-1, LANES)  151 us
    all_gather x2, blocking collectives, fetch_feed(): lax.all_gather(shortened(flatten_all(params)), ('dp', 'fsdp'), axis=0, ti...  147 us
    reshape x24, local copies, waits for them, and re-layouts, restore_all(): item.reshape(-1, width)  143 us
    dot_general x24, matrix products, against(): lax.dot_general(left, right, (((1,), (1,)), ((), ())), preferred_element_...  130 us
  transfers between devices with their start and end apart: 22, of which 12 were waited for; matrix products, arithmetic and copies ran while one was open for 18% of the time, Pallas kernels for 0%

commit v1 on v0

v1 whole, which is shorter than its diff:
```python
import jax
import jax.numpy as jnp
from jax import lax
from jax.sharding import PartitionSpec as P

EPSILON = 1e-06
THETA = 10000.0
LANES = 128
HDIM = 256
BOTH = ("dp", "fsdp")
BF16 = jnp.bfloat16
F32 = jnp.float32


def product(left, right):
    return jnp.dot(left, right, preferred_element_type=F32)


def contract_rows(left, right):
    return lax.dot_general(left, right, (((0,), (0,)), ((), ())), preferred_element_type=F32)


def against(left, right):
    return lax.dot_general(left, right, (((1,), (1,)), ((), ())), preferred_element_type=F32)


def rotation(positions, width):
    halfway = width // 2
    frequency = jnp.power(THETA, -2.0 * jnp.arange(halfway, dtype=F32) / width)
    angles = positions.astype(F32)[:, None] * frequency[None, :]
    return (jnp.cos(angles), jnp.sin(angles))


def rotate(values, cosine, sine_part):
    halfway = values.shape[-1] // 2
    leading = values[..., :halfway]
    second = values[..., halfway:]
    return jnp.concatenate(
        [leading * cosine - second * sine_part, second * cosine + leading * sine_part], axis=-1
    )


def gelu_parts(v):
    inner = 0.7978845608028654 * (v + 0.044715 * v * v * v)
    t = jnp.tanh(inner)
    value = 0.5 * v * (1.0 + t)
    slope = 0.5 * (1.0 + t) + 0.5 * v * (1.0 - t * t) * (
        0.7978845608028654 * (1.0 + 3.0 * 0.044715 * v * v)
    )
    return value, slope


def gather_packed(pieces, count):
    flat = [piece.reshape(-1, LANES) for piece in pieces]
    sizes = [f.shape[0] for f in flat]
    packed = jnp.concatenate(flat, axis=0)
    spare = -packed.shape[0] % 8
    packed = jnp.pad(packed, ((0, spare), (0, 0)))
    full = lax.all_gather(packed, BOTH, axis=0, tiled=False)
    out, at = [], 0
    for piece, size in zip(pieces, sizes):
        part = full[:, at : at + size]
        out.append(part.reshape(count * piece.shape[0], piece.shape[1]))
        at += size
    return out


def scatter_packed(grads, count):
    flat = [g.astype(BF16).reshape(count, -1, LANES) for g in grads]
    sizes = [f.shape[1] for f in flat]
    packed = jnp.concatenate(flat, axis=1)
    spare = -packed.shape[1] % 64
    packed = jnp.pad(packed, ((0, 0), (0, spare), (0, 0)))
    rows = packed.shape[1]
    summed = lax.psum_scatter(
        packed.reshape(count * rows, LANES), BOTH, scatter_dimension=0, tiled=True
    )
    out, at = [], 0
    for g, size in zip(grads, sizes):
        out.append(summed[at : at + size].reshape(g.shape[0] // count, g.shape[1]).astype(F32))
        at += size
    return out


def per_device_of(ND, NF):
    COUNT = ND * NF

    def per_device(
        layer_input,
        output_gradient,
        prefix_length,
        attention_gain,
        inward,
        inward_down,
        inward_up,
        outward,
        outward_down,
        outward_up,
        feedforward_gain,
        widening,
        widening_down,
        widening_up,
        narrowing,
        narrowing_down,
        narrowing_up,
    ):
        micro_count, _, T, D = layer_input.shape
        QKV = inward.shape[1]
        query_width = outward.shape[0] * COUNT
        HEADS = query_width // HDIM
        FF = widening.shape[1] // 2
        RANK = widening_down.shape[1]
        FS = FF // ND
        FP = -(-FS // LANES) * LANES
        ROWS = D // COUNT
        UPS = RANK // COUNT
        scale = HDIM ** (-0.5)

        gains = jnp.pad(
            jnp.stack([attention_gain, feedforward_gain]), ((0, 0), (0, LANES - ROWS))
        )
        gains_full, inward_full, inward_down_full, inward_up_full = gather_packed(
            (gains, inward, inward_down, inward_up), COUNT
        )
        gains_full = gains_full.reshape(COUNT, 2, LANES)[:, :, :ROWS].astype(F32)
        first_gain = gains_full[:, 0].reshape(D)
        second_gain = gains_full[:, 1].reshape(D)
        (
            outward_full,
            outward_down_full,
            outward_up_full,
            widening_down_full,
            narrowing_up_full,
        ) = gather_packed((outward, outward_down, outward_up, widening_down, narrowing_up), COUNT)

        wide = jnp.concatenate([widening, widening_up], axis=0)
        wide = wide.reshape(ROWS + UPS, 2, ND, FS)
        wide = jnp.pad(wide, ((0, 0), (0, 0), (0, 0), (0, FP - FS)))
        wide = wide.transpose(2, 0, 1, 3).reshape(ND, ROWS + UPS, 2 * FP)
        wide = lax.all_to_all(wide, "dp", 0, 0, tiled=True)
        wide = lax.all_gather(wide, "fsdp", axis=0, tiled=False)
        wide = wide.transpose(1, 0, 2, 3)
        widening_slice = wide[:, :, :ROWS].reshape(D, 2 * FP)
        widening_up_slice = wide[:, :, ROWS:].reshape(RANK, 2 * FP)
        narrow = jnp.concatenate([narrowing, narrowing_down], axis=1)
        narrow = lax.all_gather(narrow, "fsdp", axis=0, tiled=True)
        narrow = jnp.pad(narrow, ((0, FP - FS), (0, 0)))
        narrowing_slice, narrowing_down_slice = narrow[:, :D], narrow[:, D:]

        inward_eff = (inward_full + product(inward_down_full, inward_up_full)).astype(BF16)
        outward_eff = (outward_full + product(outward_down_full, outward_up_full)).astype(BF16)
        wide_eff = (widening_slice + product(widening_down_full, widening_up_slice)).astype(BF16)
        narrow_eff = (narrowing_slice + product(narrowing_down_slice, narrowing_up_full)).astype(
            BF16
        )

        positions = lax.axis_index("fsdp") * T + jnp.arange(T, dtype=jnp.int32)
        cosine, sine_part = rotation(positions, HDIM)
        head_cosine = cosine[:, None, :]
        head_sine = sine_part[:, None, :]

        def unit(v):
            return v * lax.rsqrt(jnp.mean(v * v, axis=-1, keepdims=True) + EPSILON)

        def unit_back(v, gain, upstream):
            r = lax.rsqrt(jnp.mean(v * v, axis=-1, keepdims=True) + EPSILON)
            n = v * r
            e = upstream * gain
            back = r * (e - n * jnp.mean(e * n, axis=-1, keepdims=True))
            return back, jnp.sum(upstream * n, axis=0)

        micro = range(micro_count)
        residual = [layer_input[m, 0].astype(F32) for m in micro]
        upstream = [output_gradient[m, 0] for m in micro]
        upstream_all = [lax.all_gather(g, "dp", axis=0, tiled=True) for g in upstream]

        normed_first, queries, all_keys, all_values = [], [], [], []
        visible, logsum, mixed, middle, normed_second = [], [], [], [], []
        second_all = []

        def masked_scores(m):
            raw = (
                jnp.einsum("rhd,kd->hrk", queries[m], all_keys[m], preferred_element_type=F32)
                * scale
            )
            return jnp.where(visible[m][None], raw, -1e30)

        for m in micro:
            h1 = (unit(residual[m]) * first_gain).astype(BF16)
            normed_first.append(h1)
            joint = product(h1, inward_eff)
            queries.append(
                rotate(
                    joint[:, :query_width].reshape(T, HEADS, HDIM), head_cosine, head_sine
                ).astype(BF16)
            )
            own_keys = rotate(joint[:, query_width : query_width + HDIM], cosine, sine_part)
            own = jnp.concatenate([own_keys, joint[:, query_width + HDIM :]], axis=1).astype(BF16)
            both = lax.all_gather(own, "fsdp", axis=0, tiled=True)
            all_keys.append(both[:, :HDIM])
            all_values.append(both[:, HDIM:])
            key_pos = jnp.arange(NF * T, dtype=jnp.int32)
            limit = prefix_length[m, 0]
            visible.append(
                (key_pos[None, :] <= positions[:, None]) | (key_pos[None, :] < limit)
            )
            scores = masked_scores(m)
            peak = jnp.max(scores, axis=-1, keepdims=True)
            total = jnp.sum(jnp.exp(scores - peak), axis=-1, keepdims=True)
            logsum.append(peak + jnp.log(total))
            probs_low = jnp.exp(scores - logsum[m]).astype(BF16)
            mix = jnp.einsum("hrk,kd->rhd", probs_low, all_values[m], preferred_element_type=F32)
            mixed.append(mix.reshape(T, query_width).astype(BF16))
            middle.append(residual[m] + product(mixed[m], outward_eff))
            normed_second.append((unit(middle[m]) * second_gain).astype(BF16))
            second_all.append(lax.all_gather(normed_second[m], "dp", axis=0, tiled=True))

        outputs, middle_grad = [], []
        wide_grad = narrow_grad = None
        second_gain_grad = 0.0
        for m in micro:
            spread = product(second_all[m], wide_eff)
            gate, upper = spread[:, :FP], spread[:, FP:]
            value, slope = gelu_parts(gate)
            activated = (value * upper).astype(BF16)
            shrink = product(activated, narrow_eff).astype(BF16)
            shrink = lax.psum_scatter(shrink, "dp", scatter_dimension=0, tiled=True)
            outputs.append((middle[m] + shrink.astype(F32)).astype(BF16))
            act_grad = against(upstream_all[m], narrow_eff)
            spread_grad = jnp.concatenate(
                [act_grad * upper * slope, act_grad * value], axis=1
            ).astype(BF16)
            rows_grad = against(spread_grad, wide_eff).astype(BF16)
            rows_grad = lax.psum_scatter(rows_grad, "dp", scatter_dimension=0, tiled=True)
            part = contract_rows(activated, upstream_all[m])
            narrow_grad = part if narrow_grad is None else narrow_grad + part
            part = contract_rows(second_all[m], spread_grad)
            wide_grad = part if wide_grad is None else wide_grad + part
            back, gain_grad = unit_back(middle[m], second_gain, rows_grad.astype(F32))
            second_gain_grad = second_gain_grad + gain_grad
            middle_grad.append(upstream[m].astype(F32) + back)

        wide_grad = wide_grad.astype(BF16)
        narrow_grad = narrow_grad.astype(BF16)
        wide_up_grad = contract_rows(widening_down_full, wide_grad).astype(BF16)
        widening_down_part = against(wide_grad, widening_up_slice)
        narrowing_up_part = contract_rows(narrowing_down_slice, narrow_grad)
        wide_both = jnp.concatenate(
            [
                wide_grad.reshape(ND, NF, ROWS, 2 * FP),
                wide_up_grad.reshape(ND, NF, UPS, 2 * FP),
            ],
            axis=2,
        ).transpose(1, 0, 2, 3)
        wide_both = wide_both.reshape(NF * ND * (ROWS + UPS), 2 * FP)
        wide_both = lax.psum_scatter(wide_both, "fsdp", scatter_dimension=0, tiled=True)
        wide_both = wide_both.reshape(ND, ROWS + UPS, 2 * FP)
        wide_both = lax.all_to_all(wide_both, "dp", 0, 0, tiled=True)
        wide_both = wide_both.reshape(ND, ROWS + UPS, 2, FP)[..., :FS].transpose(1, 2, 0, 3)
        wide_both = wide_both.reshape(ROWS + UPS, 2 * FF).astype(F32)
        widening_grad, widening_up_grad = wide_both[:ROWS], wide_both[ROWS:]
        narrow_sum = lax.psum_scatter(
            narrow_grad[:FS], "fsdp", scatter_dimension=0, tiled=True
        )
        narrowing_grad = narrow_sum.astype(F32)
        narrowing_down_grad = against(narrow_sum, narrowing_up_full)

        branch_grad, joint_grads, mixed_grads = [], [], []
        for m in micro:
            branch_grad.append(middle_grad[m].astype(BF16))
        outward_part = contract_rows(
            jnp.concatenate(mixed, axis=0), jnp.concatenate(branch_grad, axis=0)
        ).astype(BF16)
        outward_up_part = contract_rows(outward_down_full, outward_part)
        (
            outward_grad,
            outward_up_grad,
            widening_down_grad,
            narrowing_up_grad,
        ) = scatter_packed(
            (outward_part, outward_up_part, widening_down_part, narrowing_up_part), COUNT
        )
        outward_down_grad = against(outward_grad.astype(BF16), outward_up_full)

        input_grads = []
        first_gain_grad = 0.0
        for m in micro:
            mixed_grad = against(branch_grad[m], outward_eff).astype(BF16)
            mixed_grad = mixed_grad.reshape(T, HEADS, HDIM)
            probs_again = jnp.exp(masked_scores(m) - logsum[m])
            prob_grad = jnp.einsum(
                "rhd,kd->hrk", mixed_grad, all_values[m], preferred_element_type=F32
            )
            center = jnp.sum(probs_again * prob_grad, axis=-1, keepdims=True)
            score_grad = (probs_again * (prob_grad - center)).astype(BF16)
            query_grad = (
                jnp.einsum("hrk,kd->rhd", score_grad, all_keys[m], preferred_element_type=F32)
                * scale
            )
            key_grad = (
                jnp.einsum("hrk,rhd->kd", score_grad, queries[m], preferred_element_type=F32)
                * scale
            )
            value_grad = jnp.einsum(
                "hrk,rhd->kd", probs_again.astype(BF16), mixed_grad, preferred_element_type=F32
            )
            both = jnp.concatenate([key_grad, value_grad], axis=1).astype(BF16)
            both = lax.psum_scatter(both, "fsdp", scatter_dimension=0, tiled=True).astype(F32)
            joint_grads.append(
                jnp.concatenate(
                    [
                        rotate(query_grad, head_cosine, -head_sine).reshape(T, query_width),
                        rotate(both[:, :HDIM], cosine, -sine_part),
                        both[:, HDIM:],
                    ],
                    axis=1,
                ).astype(BF16)
            )
            first_rows_grad = against(joint_grads[m], inward_eff)
            back, gain_grad = unit_back(residual[m], first_gain, first_rows_grad)
            first_gain_grad = first_gain_grad + gain_grad
            input_grads.append(middle_grad[m] + back)

        inward_part = contract_rows(
            jnp.concatenate(normed_first, axis=0), jnp.concatenate(joint_grads, axis=0)
        ).astype(BF16)
        inward_up_part = contract_rows(inward_down_full, inward_part)
        gain_parts = jnp.stack([first_gain_grad, second_gain_grad]).reshape(2, COUNT, ROWS)
        gain_parts = jnp.pad(gain_parts, ((0, 0), (0, 0), (0, LANES - ROWS)))
        gain_parts = gain_parts.transpose(1, 0, 2).reshape(COUNT * 2, LANES)
        inward_grad, inward_up_grad, gain_grads = scatter_packed(
            (inward_part, inward_up_part, gain_parts), COUNT
        )
        inward_down_grad = against(inward_grad.astype(BF16), inward_up_full)

        return (
            jnp.stack(outputs)[:, None],
            jnp.stack(input_grads)[:, None],
            gain_grads[0, :ROWS],
            inward_grad,
            inward_down_grad,
            inward_up_grad,
            outward_grad,
            outward_down_grad,
            outward_up_grad,
            gain_grads[1, :ROWS],
            widening_grad,
            widening_down_grad,
            widening_up_grad,
            narrowing_grad,
            narrowing_down_grad,
            narrowing_up_grad,
        )

    return per_device


def solution(mesh):
    rows = P(BOTH, None)
    tokens = P(None, "dp", "fsdp", None)
    weights = (P(BOTH),) + (rows,) * 6 + (P(BOTH),) + (rows,) * 6
    return jax.shard_map(
        per_device_of(mesh.shape["dp"], mesh.shape["fsdp"]),
        mesh=mesh,
        in_specs=(tokens, tokens, P(None, "dp")) + weights,
        out_specs=(tokens, tokens) + weights,
        check_vma=False,
    )
```

time: 3140 us -> 1270 us (0.40)
  waiting for transfers between devices: 1720 us -> 746 us
  blocking collectives: 613 us -> 29.8 us
  matrix products: 426 us -> 241 us
  local copies, waits for them, and re-layouts: 330 us -> 149 us
  other arithmetic: 23.9 us -> 74.6 us
    unnamed x28 -> x21, waiting for transfers between devices: 1000 us -> 1.01 us
    all_gather x10 -> x0, blocking collectives: 531 us -> none  [the longest x4 317 us: fetch_attention(): lax.all_gather(shortened(flatten_all(params)), ('dp', 'fsdp'), axis=0, ti...]
    all_gather x6 -> x10, waiting for transfers between devices: 0.05 us -> 286 us  [the longest x1 81.3 us: per_device(): wide = lax.all_gather(wide, 'fsdp', axis=0, tiled=False)]
    reduce_scatter x10 -> x9, waiting for transfers between devices: 717 us -> 442 us  [the longest x2 224 us: scatter_packed(): lax.psum_scatter(packed.reshape(count * rows, LANES), BOTH, scatter_dimen...]
    reshape x50 -> x33, local copies, waits for them, and re-layouts: 297 us -> 53.6 us  [the longest x6 16.6 us: scatter_packed(): flat = [g.astype(BF16).reshape(count, -1, LANES) for g in grads]]
    dot_general x24 -> x10, matrix products: 164 us -> 67.2 us  [contract_rows(): lax.dot_general(left, right, (((0,), (0,)), ((), ())), preferred_element_...]
    unnamed x2 -> x0, blocking collectives: 81.5 us -> none
    dot_general x24 -> x12, matrix products: 130 us -> 76.3 us  [against(): lax.dot_general(left, right, (((1,), (1,)), ((), ())), preferred_element_...]
  transfers between devices with their start and end apart: 22 -> 21, of which waited for: 12 -> 15; matrix products, arithmetic and copies ran while one was open for 18% -> 31% of each run, Pallas kernels for 0% -> 0%
where the time goes in v1:
time: 1270 us; the launch traced here: 1260 us
  waiting for transfers between devices  746 us (59%)
  matrix products  241 us (19%)
  local copies, waits for them, and re-layouts  149 us (12%)
  other arithmetic  74.6 us (6%)
  blocking collectives  29.8 us (2%)
  between operations  16.3 us (1%)
    reduce_scatter x2, waiting for transfers between devices, scatter_packed(): lax.psum_scatter(packed.reshape(count * rows, LANES), BOTH, scatter_dimen...  224 us
    reduce_scatter x2, waiting for transfers between devices, per_device(): lax.psum_scatter(rows_grad, 'dp', scatter_dimension=0, tiled=True)  91.5 us
    all_gather x1, waiting for transfers between devices, per_device(): wide = lax.all_gather(wide, 'fsdp', axis=0, tiled=False)  81.3 us
    dot_general x12, matrix products, against(): lax.dot_general(left, right, (((1,), (1,)), ((), ())), preferred_element_...  76.3 us
    dot_general x12, matrix products, product(): return jnp.dot(left, right, preferred_element_type=F32)  73.4 us
    reduce_scatter x1, waiting for transfers between devices, per_device(): lax.psum_scatter(wide_both, 'fsdp', scatter_dimension=0, tiled=True)  72.2 us
    dot_general x10, matrix products, contract_rows(): lax.dot_general(left, right, (((0,), (0,)), ((), ())), preferred_element_...  67.2 us
    all_gather x2, waiting for transfers between devices, per_device(): lax.all_gather(normed_second[m], 'dp', axis=0, tiled=True)  65.1 us
  transfers between devices with their start and end apart: 21, of which 15 were waited for; matrix products, arithmetic and copies ran while one was open for 31% of the time, Pallas kernels for 0%

profile of v1, /device:TPU:0, one launch (start us, length us, event | category | flops | bytes accessed | tf_op | source)
XLA Modules:
  0.0 1264.0 jit_solution(12420063974194455569)
XLA Ops:
  17.8 60.9 %all-gather.26.cloned.1.call-done = bf16[19456,128]{1,0:T(8,128)(2,1)} async-done(((bf16[608,128]{1,0:T(8,128)(2,1)}), bf16[19456,128]{1,0:T(8,128)(2,1)}) %all-gather.26.cloned.1.call-update) | async-done | bytes 4980752 | tf_op jit(solution)/shard_map/all_gather | solution.py:59
  90.2 8.4 reshape.496
  114.7 29.8 %all_to_all.10 = bf16[8,44,1792]{2,1,0:T(8,128)(2,1)S(1)} all-to-all(bf16[8,44,1792]{2,1,0:T(8,128)(2,1)S(1)} %copy.157), channel_id=1, replica_groups=mesh['dp'=8,'fsdp'=4] {'dp'}, dimensions={0} | all-to-all | bytes 2523136 | tf_op jit(solution)/shard_map/all_to_all | solution.py:140
  195.8 81.3 %all-gather.30.cloned.1.call-done = bf16[32,44,1792]{2,0,1:T(8,128)(2,1)} async-done(((bf16[8,44,1792]{2,0,1:T(8,128)(2,1)}), bf16[32,44,1792]{2,0,1:T(8,128)(2,1)}) %all-gather.30.cloned.1.call-update) | async-done | bytes 5046288 | tf_op jit(solution)/shard_map/all_gather | solution.py:141
  282.4 8.4 copy.159
  290.8 9.3 reshape.498
  301.9 26.4 %all-gather.20.cloned.1.call-done = bf16[864,1408]{1,0:T(8,128)(2,1)} async-done(((bf16[216,1408]{1,0:T(8,128)(2,1)}), bf16[864,1408]{1,0:T(8,128)(2,1)}) %all-gather.20.cloned.1.call-update) | async-done | bytes 2433040 | tf_op jit(solution)/shard_map/all_gather | solution.py:146
  341.1 27.0 %all-gather.18.cloned.1.call-done = bf16[2048,1152]{1,0:T(8,128)(2,1)} async-done(((bf16[256,1152]{1,0:T(8,128)(2,1)}), bf16[2048,1152]{1,0:T(8,128)(2,1)}) %all-gather.18.cloned.1.call-update) | async-done | bytes 4718608 | tf_op jit(solution)/shard_map/all_gather | solution.py:216
  368.1 15.7 %fusion.226 = f32[2048,1792]{0,1:T(8,128)} fusion(bf16[2048,1152]{1,0:T(8,128)(2,1)} %all-gather.18.cloned.1.call-done, bf16[1152,1792]{1,0:T(8,128)(2,1)} %fusion.9), kind=kOutput, calls=%fused_computation.357 | convolution fusion | flops 8455716864 | bytes 23527424 | tf_op jit(solution)/shard_map/dot_general | solution.py:16
  383.8 25.6 %all-gather.32.cloned.1.call-done = bf16[1,1,2048,1152]{3,2,1,0:T(8,128)(2,1)} async-done(((bf16[1,1,256,1152]{3,2,1,0:T(8,128)(2,1)}), bf16[1,1,2048,1152]{3,2,1,0:T(8,128)(2,1)}) %all-gather.32.cloned.1.call-update) | async-done | bytes 4718608 | tf_op jit(solution)/shard_map/all_gather | solution.py:175
  409.4 15.2 %fusion.19 = (bf16[2048,896]{0,1:T(8,128)(2,1)S(1)}, bf16[2048,896]{0,1:T(8,128)(2,1)}, bf16[2048,896]{0,1:T(8,128)(2,1)}) fusion(f32[2048,1792]{0,1:T(8,128)} %fusion.226, bf16[896,1152]{1,0:T(8,128)(2,1)S(1)} %copy-done.48, bf16[1,1,2048,1152]{3,2,1,0:T(8,128)(2,1)} %all-gather.32.cloned.1.call-done), kind=kOutput, calls=%fused_computation.33 | convolution fusion | flops 4273733632 | bytes 32473088 | tf_op jit(solution)/shard_map/dot_general | solution.py:24
  426.4 13.0 %convolution_convert_fusion.3 = bf16[2048,1152]{1,0:T(8,128)(2,1)} fusion(bf16[1152,1792]{1,0:T(8,128)(2,1)S(1)} %copy-done.36, bf16[2048,896]{0,1:T(8,128)(2,1)} %get-tuple-element.95, bf16[2048,896]{0,1:T(8,128)(2,1)S(1)} %get-tuple-element.94), kind=kOutput, calls=%fused_computation.21 | convolution fusion | flops 8472756224 | bytes 16187392 | tf_op jit(solution)/shard_map/dot_general | solution.py:24
  447.4 48.7 %reduce-scatter.17.cloned.1.call-done = bf16[256,1152]{1,0:T(8,128)(2,1)} async-done(((bf16[2048,1152]{1,0:T(8,128)(2,1)}), bf16[256,1152]{1,0:T(8,128)(2,1)}) %reduce-scatter.17.cloned.1.call-update) | async-done | bytes 589840 | tf_op jit(solution)/shard_map/reduce_scatter | solution.py:234
  499.9 38.2 %all-gather.24.cloned.1.call-done = bf16[2048,1152]{1,0:T(8,128)(2,1)} async-done(((bf16[256,1152]{1,0:T(8,128)(2,1)}), bf16[2048,1152]{1,0:T(8,128)(2,1)}) %all-gather.24.cloned.1.call-update) | async-done | bytes 4718608 | tf_op jit(solution)/shard_map/all_gather | solution.py:216
  538.1 15.9 %fusion.228 = f32[2048,1792]{0,1:T(8,128)} fusion(bf16[2048,1152]{1,0:T(8,128)(2,1)} %all-gather.24.cloned.1.call-done, bf16[1152,1792]{1,0:T(8,128)(2,1)} %fusion.9), kind=kOutput, calls=%fused_computation.359 | convolution fusion | flops 8455716864 | bytes 23527424 | tf_op jit(solution)/shard_map/dot_general | solution.py:16
  554.0 24.8 %all-gather.34.cloned.1.call-done = bf16[1,1,2048,1152]{3,2,1,0:T(8,128)(2,1)} async-done(((bf16[1,1,256,1152]{3,2,1,0:T(8,128)(2,1)}), bf16[1,1,2048,1152]{3,2,1,0:T(8,128)(2,1)}) %all-gather.34.cloned.1.call-update) | async-done | bytes 4718608 | tf_op jit(solution)/shard_map/all_gather | solution.py:175
  578.8 17.2 %fusion.25 = (bf16[2048,896]{0,1:T(8,128)(2,1)S(1)}, bf16[2048,896]{0,1:T(8,128)(2,1)}, bf16[2048,896]{0,1:T(8,128)(2,1)}) fusion(f32[2048,1792]{0,1:T(8,128)} %fusion.228, bf16[896,1152]{1,0:T(8,128)(2,1)} %fusion.52, bf16[1,1,2048,1152]{3,2,1,0:T(8,128)(2,1)} %all-gather.34.cloned.1.call-done), kind=kOutput, calls=%fused_computation.39 | convolution fusion | flops 4273733632 | bytes 32473088 | tf_op jit(solution)/shard_map/dot_general | solution.py:24
  597.8 13.3 %convolution_convert_fusion.2 = bf16[2048,1152]{1,0:T(8,128)(2,1)} fusion(bf16[1152,1792]{1,0:T(8,128)(2,1)S(1)} %copy-done.37, bf16[2048,896]{0,1:T(8,128)(2,1)} %get-tuple-element.97, bf16[2048,896]{0,1:T(8,128)(2,1)S(1)} %get-tuple-element.96), kind=kOutput, calls=%fused_computation.20 | convolution fusion | flops 8472756224 | bytes 16187392 | tf_op jit(solution)/shard_map/dot_general | solution.py:24
  611.1 9.4 convolution_convert_fusion
  622.2 42.8 %reduce-scatter.21.cloned.1.call-done = bf16[256,1152]{1,0:T(8,128)(2,1)} async-done(((bf16[2048,1152]{1,0:T(8,128)(2,1)}), bf16[256,1152]{1,0:T(8,128)(2,1)}) %reduce-scatter.21.cloned.1.call-update) | async-done | bytes 589840 | tf_op jit(solution)/shard_map/reduce_scatter | solution.py:234
  667.7 54.6 %reduce-scatter.15.cloned.1.call-done = bf16[256,1152]{1,0:T(8,128)(2,1)} async-done(((bf16[2048,1152]{1,0:T(8,128)(2,1)}), bf16[256,1152]{1,0:T(8,128)(2,1)}) %reduce-scatter.15.cloned.1.call-update) | async-done | bytes 589840 | tf_op jit(solution)/shard_map/reduce_scatter | solution.py:227
  748.3 8.5 fusion.31
  756.9 7.6 fusion.53
  768.1 10.1 convolution_convert_fusion.1
  778.7 16.2 %fusion.28 = f32[1152,1792]{1,0:T(8,128)} fusion(bf16[2048,1152]{1,0:T(8,128)(2,1)} %all-gather.18.cloned.1.call-done, bf16[2048,896]{0,1:T(8,128)(2,1)} %get-tuple-element.95, bf16[2048,896]{0,1:T(8,128)(2,1)} %copy-done.105), kind=kOutput, calls=%fused_computation.54 | convolution fusion | flops 8470396928 | bytes 20316160 | tf_op jit(solution)/shard_map/dot_general | solution.py:20
  794.8 16.0 %fusion.7 = bf16[1152,1792]{1,0:T(8,128)(2,1)} fusion(f32[1152,1792]{1,0:T(8,128)} %fusion.28, bf16[2048,1152]{1,0:T(8,128)(2,1)} %all-gather.24.cloned.1.call-done, bf16[2048,896]{0,1:T(8,128)(2,1)} %get-tuple-element.97, bf16[2048,896]{0,1:T(8,128)(2,1)S(1)} %copy-done.107), kind=kOutput, calls=%fused_computation.18 | convolution fusion | flops 8474525696 | bytes 24444928 | tf_op jit(solution)/shard_map/dot_general | solution.py:20
  810.8 7.1 reshape.490
  825.2 7.4 reshape.492
  912.9 72.2 %reduce-scatter.29.cloned.1.call-done = bf16[352,1792]{1,0:T(8,128)(2,1)} async-done(((bf16[1408,1792]{1,0:T(8,128)(2,1)}), bf16[352,1792]{1,0:T(8,128)(2,1)}) %reduce-scatter.29.cloned.1.call-update) | async-done | bytes 1261584 | tf_op jit(solution)/shard_map/reduce_scatter | solution.py:256
  996.5 17.0 %all-to-all-done.1 = bf16[8,44,1792]{2,1,0:T(8,128)(2,1)} async-done(((bf16[8,44,1792]{2,1,0:T(8,128)(2,1)}), bf16[8,44,1792]{2,1,0:T(8,128)(2,1)}, u32[]{:S(2)}, u32[]{:S(2)}) %all-to-all-start.1) | async-done | bytes 1261600 | tf_op jit(solution)/shard_map/all_to_all | solution.py:258
  1022.2 115.4 %reduce-scatter.27.cloned.1.call-done = bf16[512,128]{1,0:T(8,128)(2,1)} async-done(((bf16[16384,128]{1,0:T(8,128)(2,1)}), bf16[512,128]{1,0:T(8,128)(2,1)}) %reduce-scatter.27.cloned.1.call-update) | async-done | bytes 131088 | tf_op jit(solution)/shard_map/reduce_scatter | solution.py:75
  1140.2 108.7 %reduce-scatter.25.cloned.1.call-done = bf16[576,128]{1,0:T(8,128)(2,1)} async-done(((bf16[18432,128]{1,0:T(8,128)(2,1)}), bf16[576,128]{1,0:T(8,128)(2,1)}) %reduce-scatter.25.cloned.1.call-update) | async-done | bytes 147472 | tf_op jit(solution)/shard_map/reduce_scatter | solution.py:75
  (447 shorter events, 275.8 us)
Async XLA Ops:
  7.2 71.5 %all-gather.26.cloned.1.call-start = ((), (), s32[]{:S(2)}) async-start(), calls=%async_computation.26 | async-start | bytes 5136384 | tf_op jit(solution)/shard_map/all_gather | solution.py:59
  11.3 140.8 %all-gather.28.cloned.1.call-start = ((), (), s32[]{:S(2)}) async-start(), calls=%async_computation.27 | async-start | bytes 4798464 | tf_op jit(solution)/shard_map/all_gather | solution.py:59
  16.1 169.3 %all-gather.16.cloned.1.call-start = ((), (), s32[]{:S(2)}) async-start(), calls=%async_computation.12 | async-start | bytes 1310720 | tf_op jit(solution)/shard_map/all_gather | solution.py:199
  16.2 89.8 %copy-start.101 = (f32[128]{0:T(128)}, f32[128]{0:T(128)S(1)}, u32[]{:S(2)}) copy-start(f32[128]{0:T(128)S(1)} %multiply_power_fusion) | copy-start | bytes 1540
  16.2 89.8 %copy-start.97 = (f32[256]{0:T(256)}, f32[256]{0:T(256)S(1)}, u32[]{:S(2)}) copy-start(f32[256]{0:T(256)S(1)} %get-tuple-element.169) | copy-start | bytes 3076
  17.8 85.0 %copy-start.95 = (f32[256]{0:T(256)}, f32[256]{0:T(256)S(1)}, u32[]{:S(2)}) copy-start(f32[256]{0:T(256)S(1)} %get-tuple-element.166) | copy-start | bytes 3076
  109.2 167.9 %all-gather.30.cloned.1.call-start = ((), (), s32[]{:S(2)}) async-start(), calls=%async_computation.28 | async-start | bytes 6307840 | tf_op jit(solution)/shard_map/all_gather | solution.py:141
  146.0 182.3 %all-gather.20.cloned.1.call-start = ((), (), s32[]{:S(2)}) async-start(), calls=%async_computation.14 | async-start | bytes 3041280 | tf_op jit(solution)/shard_map/all_gather | solution.py:146
  147.0 221.1 %all-gather.18.cloned.1.call-start = ((), (), s32[]{:S(2)}) async-start(), calls=%async_computation.13 | async-start | bytes 5308416 | tf_op jit(solution)/shard_map/all_gather | solution.py:216
  181.8 540.5 %copy-start.70 = (f32[1152]{0:T(1024)}, f32[1152]{0:T(1024)S(1)}, u32[]{:S(2)}) copy-start(f32[1152]{0:T(1024)S(1)} %mul.552) | copy-start | bytes 13828
  191.8 530.4 %copy-start.4 = (f32[256,1152]{1,0:T(8,128)}, f32[256,1152]{1,0:T(8,128)S(1)}, u32[]{:S(2)}) copy-start(f32[256,1152]{1,0:T(8,128)S(1)} %get-tuple-element.156) | copy-start | bytes 3538948
  191.8 304.3 %copy-start.94 = (f32[256]{0:T(256)}, f32[256]{0:T(256)S(1)}, u32[]{:S(2)}) copy-start(f32[256]{0:T(256)S(1)} %add_rsqrt_fusion.2) | copy-start | bytes 3076
  193.0 216.3 %all-gather.32.cloned.1.call-start = ((), (), s32[]{:S(2)}) async-start(), calls=%async_computation.29 | async-start | bytes 5308416 | tf_op jit(solution)/shard_map/all_gather | solution.py:175
  195.5 244.1 %all-gather.22.cloned.1.call-start = ((), (), s32[]{:S(2)}) async-start(), calls=%async_computation.16 | async-start | bytes 1310720 | tf_op jit(solution)/shard_map/all_gather | solution.py:199
  340.6 155.6 %reduce-scatter.17.cloned.1.call-start = ((), (), s32[]{:S(2)}) async-start(), calls=%async_computation.19 | async-start | bytes 5308416 | tf_op jit(solution)/shard_map/reduce_scatter | solution.py:234
  439.5 98.6 %all-gather.24.cloned.1.call-start = ((), (), s32[]{:S(2)}) async-start(), calls=%async_computation.17 | async-start | bytes 5308416 | tf_op jit(solution)/shard_map/all_gather | solution.py:216
  447.4 274.9 %copy-start.6 = (f32[256,1152]{1,0:T(8,128)}, f32[256,1152]{1,0:T(8,128)S(1)}, u32[]{:S(2)}) copy-start(f32[256,1152]{1,0:T(8,128)S(1)} %get-tuple-element.160) | copy-start | bytes 3538948
  447.4 274.8 %copy-start.93 = (f32[256]{0:T(256)}, f32[256]{0:T(256)S(1)}, u32[]{:S(2)}) copy-start(f32[256]{0:T(256)S(1)} %add_rsqrt_fusion) | copy-start | bytes 3076
  499.2 79.7 %all-gather.34.cloned.1.call-start = ((), (), s32[]{:S(2)}) async-start(), calls=%async_computation.30 | async-start | bytes 5308416 | tf_op jit(solution)/shard_map/all_gather | solution.py:175
  499.9 165.1 %reduce-scatter.21.cloned.1.call-start = ((), (), s32[]{:S(2)}) async-start(), calls=%async_computation.21 | async-start | bytes 5308416 | tf_op jit(solution)/shard_map/reduce_scatter | solution.py:234
  611.1 111.2 %reduce-scatter.15.cloned.1.call-start = ((), (), s32[]{:S(2)}) async-start(), calls=%async_computation.18 | async-start | bytes 5308416 | tf_op jit(solution)/shard_map/reduce_scatter | solution.py:227
  620.5 101.8 %copy-start.18 = (bf16[2,1,256,1152]{3,2,1,0:T(8,128)(2,1)S(1)}, bf16[2,1,256,1152]{3,2,1,0:T(8,128)(2,1)}, u32[]{:S(2)}) copy-start(bf16[2,1,256,1152]{3,2,1,0:T(8,128)(2,1)} %param.18) | copy-start | bytes 3538948
  620.5 245.6 %reduce-scatter.19.cloned.1.call-start = ((), (), s32[]{:S(2)}) async-start(), calls=%async_computation.20 | async-start | bytes 1310720 | tf_op jit(solution)/shard_map/reduce_scatter | solution.py:308
  737.0 130.2 %reduce-scatter.23.cloned.1.call-start = ((), (), s32[]{:S(2)}) async-start(), calls=%async_computation.22 | async-start | bytes 1310720 | tf_op jit(solution)/shard_map/reduce_scatter | solution.py:308
  748.1 154.5 %reduce-scatter.31.cloned.1.call-start = ((), (), s32[]{:S(2)}) async-start(), calls=%async_computation.31 | async-start | bytes 2488320
  767.2 141.1 %reduce-scatter.13.cloned.1.call-start = ((), (), s32[]{:S(2)}) async-start(), calls=%async_computation.15 | async-start | bytes 5308416 | tf_op jit(solution)/shard_map/reduce_scatter | solution.py:227
  778.2 206.9 %reduce-scatter.29.cloned.1.call-start = ((), (), s32[]{:S(2)}) async-start(), calls=%async_computation.25 | async-start | bytes 6307840 | tf_op jit(solution)/shard_map/reduce_scatter | solution.py:256
  832.7 304.9 %reduce-scatter.27.cloned.1.call-start = ((), (), s32[]{:S(2)}) async-start(), calls=%async_computation.24 | async-start | bytes 4325376 | tf_op jit(solution)/shard_map/reduce_scatter | solution.py:75
  859.1 389.8 %reduce-scatter.25.cloned.1.call-start = ((), (), s32[]{:S(2)}) async-start(), calls=%async_computation.23 | async-start | bytes 4866048 | tf_op jit(solution)/shard_map/reduce_scatter | solution.py:75
  987.4 26.1 %all-to-all-start.1 = ((bf16[8,44,1792]{2,1,0:T(8,128)(2,1)}), bf16[8,44,1792]{2,1,0:T(8,128)(2,1)}, u32[]{:S(2)}, u32[]{:S(2)}) async-start(bf16[8,44,1792]{2,1,0:T(8,128)(2,1)} %reshape.493), calls=%async_computation.10 | async-start | bytes 2752512 | tf_op jit(solution)/shard_map/all_to_all | solution.py:258
  1017.7 121.6 %copy-start.28 = (bf16[256,1152]{1,0:T(8,128)(2,1)S(1)}, bf16[256,1152]{1,0:T(8,128)(2,1)}, u32[]{:S(2)}) copy-start(bf16[256,1152]{1,0:T(8,128)(2,1)} %copy-done.27) | copy-start | bytes 1769476
  1017.7 232.3 %copy-start.25 = (bf16[256,1536]{1,0:T(8,128)(2,1)S(1)}, bf16[256,1536]{1,0:T(8,128)(2,1)}, u32[]{:S(2)}) copy-start(bf16[256,1536]{1,0:T(8,128)(2,1)} %copy-done.24) | copy-start | bytes 2359300
  (99 other events, 877.0 us)
Sparse Core Ops, SparseCore 0:
  11.4 67.2 all-gather.25
  82.1 69.9 all-gather.27
  154.2 27.1 all-gather.15
  182.9 94.1 all-gather.29
  278.5 49.7 all-gather.19
  330.6 37.4 all-gather.17
  370.5 38.7 all-gather.31
  411.5 27.9 all-gather.21
  443.0 53.1 reduce-scatter.16
  499.3 38.7 all-gather.23
  540.0 38.7 all-gather.33
  611.2 53.7 reduce-scatter.20
  668.4 53.7 reduce-scatter.14
  737.1 27.3 reduce-scatter.18
  767.2 25.7 reduce-scatter.22
  795.2 40.4 reduce-scatter.30
  838.9 53.3 reduce-scatter.12
  894.5 90.5 reduce-scatter.28
  987.4 150.1 reduce-scatter.26
  1142.9 105.9 reduce-scatter.24

commit v2 on v1

v2 whole, which is shorter than its diff:
```python
import functools

import jax
import jax.numpy as jnp
from jax import lax
from jax.experimental import pallas as pl
from jax.experimental.pallas import tpu as pltpu
from jax.sharding import PartitionSpec as P

EPSILON = 1e-06
THETA = 10000.0
LANES = 128
HDIM = 256
BOTH = ("dp", "fsdp")
BF16 = jnp.bfloat16
F32 = jnp.float32


def product(left, right):
    return jnp.dot(left, right, preferred_element_type=F32)


def contract_rows(left, right):
    return lax.dot_general(left, right, (((0,), (0,)), ((), ())), preferred_element_type=F32)


def against(left, right):
    return lax.dot_general(left, right, (((1,), (1,)), ((), ())), preferred_element_type=F32)


def rotation(positions, width):
    halfway = width // 2
    frequency = jnp.power(THETA, -2.0 * jnp.arange(halfway, dtype=F32) / width)
    angles = positions.astype(F32)[:, None] * frequency[None, :]
    return (jnp.cos(angles), jnp.sin(angles))


def rotate(values, cosine, sine_part):
    halfway = values.shape[-1] // 2
    leading = values[..., :halfway]
    second = values[..., halfway:]
    return jnp.concatenate(
        [leading * cosine - second * sine_part, second * cosine + leading * sine_part], axis=-1
    )


def gelu_parts(v):
    inner = 0.7978845608028654 * (v + 0.044715 * v * v * v)
    t = jnp.tanh(inner)
    value = 0.5 * v * (1.0 + t)
    slope = 0.5 * (1.0 + t) + 0.5 * v * (1.0 - t * t) * (
        0.7978845608028654 * (1.0 + 3.0 * 0.044715 * v * v)
    )
    return value, slope


MESH = pl.DeviceIdType.MESH


def places():
    dp = lax.axis_index("dp")
    z = lax.axis_index("fsdp")
    y, x, c = dp // 4, (dp // 2) % 2, dp % 2
    at = lambda yy, xx, cc: (yy * 4 + xx * 2 + cc, z)
    return y, x, c, z, at(y, 1 - x, c), at(1 - y, x, c), at(y, x, 1 - c), dp


def hello(peer):
    pl.semaphore_signal(pltpu.get_barrier_semaphore(), inc=1, device_id=peer, device_id_type=MESH)


def greet(lines, planes, z, dp, plane_peers):
    barrier = pltpu.get_barrier_semaphore()
    base = 0
    if planes:
        base = len(plane_peers)
        for peer in plane_peers:
            hello(peer)
    if not lines:
        pl.semaphore_wait(barrier, base)
        return
    pl.when(z > 0)(lambda: hello((dp, z - 1)))
    pl.when(z < 3)(lambda: hello((dp, z + 1)))
    inner = (z > 0) & (z < 3)
    pl.when(inner)(lambda: pl.semaphore_wait(barrier, base + 2))
    pl.when(jnp.logical_not(inner))(lambda: pl.semaphore_wait(barrier, base + 1))


def remote(src, dst, send, recv, peer):
    return pltpu.make_async_remote_copy(
        src_ref=src, dst_ref=dst, send_sem=send, recv_sem=recv, device_id=peer, device_id_type=MESH
    )


def gather_body(count, lines, planes, in_ref, out_ref, local_sem, send, recv):
    y, x, c, z, to_x, to_y, to_p, dp = places()
    half = in_ref.shape[1] // 2
    low, high = pl.ds(0, half), pl.ds(half, half)
    greet(lines, planes, z, dp, (to_x, to_y, to_p))
    mine = out_ref.at[y, x, c] if planes else out_ref
    if lines:
        local = pltpu.make_async_copy(in_ref.at[0], mine.at[z], local_sem)
        steps = [(0, 1)] + [(j, side) for j in range(1, 4) for side in (-1, 1)]
    else:
        local = pltpu.make_async_copy(in_ref, mine, local_sem)
        steps = [(j, 1) for j in range(count)]
    local.start()

    def moved(kind, s, src, dst, peer):
        return remote(src, dst, send.at[kind, s], recv.at[kind, s], peer)

    def each(block):
        for j, side in steps:
            if lines and j:
                s = z + j * side
                pl.when((s >= 0) & (s <= 3))(functools.partial(block, s, j, side))
            else:
                block(z if lines else j, j, side)

    def along(s, side, src):
        return moved(0 if side < 0 else 10, s, src, mine.at[s], (dp, z - side))

    def x_of(s, src):
        return moved(1, s, src, mine.at[s], to_x)

    def y_of(s, src):
        return moved(2, s, src, mine.at[s], to_y)

    def p_of(s, src):
        return moved(3, s, src, mine.at[s], to_p)

    def first(s, j, side):
        src = in_ref.at[0 if lines else j] if not (lines and j) else mine.at[s]
        if lines:
            if j:
                along(s, side, src).wait_recv()
                pl.when((z - side >= 0) & (z - side <= 3))(lambda: along(s, side, src).start())
            else:
                pl.when(z < 3)(lambda: along(s, -1, src).start())
                pl.when(z > 0)(lambda: along(s, 1, src).start())
        if planes:
            x_of(s, src).start()
            y_of(s, src).start()
            p_of(s, src).start()

    def pair(s):
        one, two = out_ref.at[y, 1 - x, c, s], out_ref.at[1 - y, x, c, s]
        far = out_ref.at[1 - y, 1 - x, c, s]
        return (
            moved(4, s, one.at[low], one.at[low], to_y),
            moved(5, s, one, one, to_p),
            moved(6, s, two.at[high], two.at[high], to_x),
            moved(7, s, two, two, to_p),
            moved(8, s, far.at[low], far.at[low], to_p),
            moved(9, s, far.at[high], far.at[high], to_p),
        )

    def second(s, j, side):
        copies = pair(s)
        x_of(s, mine.at[s]).wait_recv()
        copies[0].start()
        copies[1].start()
        y_of(s, mine.at[s]).wait_recv()
        copies[2].start()
        copies[3].start()

    def third(s, j, side):
        copies = pair(s)
        copies[0].wait_recv()
        copies[4].start()
        copies[2].wait_recv()
        copies[5].start()

    def last(s, j, side):
        src = mine.at[s]
        if lines:
            if j:
                pl.when((z - side >= 0) & (z - side <= 3))(lambda: along(s, side, src).wait_send())
            else:
                pl.when(z < 3)(lambda: along(s, -1, src).wait_send())
                pl.when(z > 0)(lambda: along(s, 1, src).wait_send())
        if planes:
            copies = pair(s)
            p_of(s, src).wait_recv()
            for k in (1, 3, 4, 5):
                copies[k].wait_recv()
            for copy in (x_of(s, src), y_of(s, src), p_of(s, src)) + copies:
                copy.wait_send()

    each(first)
    if planes:
        each(second)
        each(third)
    each(last)
    local.wait()


def gather(own, lines, planes, identity):
    count = 4 if lines else own.shape[0]
    shape = ((2, 2, 2) if planes else ()) + (count,) + own.shape[1:]
    return pl.pallas_call(
        functools.partial(gather_body, count, lines, planes),
        out_shape=jax.ShapeDtypeStruct(shape, own.dtype),
        in_specs=[pl.BlockSpec(memory_space=pl.ANY)],
        out_specs=pl.BlockSpec(memory_space=pl.ANY),
        scratch_shapes=[
            pltpu.SemaphoreType.DMA,
            pltpu.SemaphoreType.DMA((11, count)),
            pltpu.SemaphoreType.DMA((11, count)),
        ],
        compiler_params=pltpu.CompilerParams(collective_id=identity, has_side_effects=True),
    )(own)


def add_rows(out, terms):
    rows = out.shape[0]
    step = 32 if rows % 32 == 0 else 16 if rows % 16 == 0 else 8

    def one(i, _):
        at = pl.ds(pl.multiple_of(i * step, step), step)
        total = terms[0][at].astype(F32)
        for term in terms[1:]:
            total = total + term[at].astype(F32)
        out[at] = total.astype(out.dtype)
        return 0

    lax.fori_loop(0, rows // step, one, 0)


def scatter_body(count, lines, in_ref, out_ref, *refs):
    own, from_p, from_y, from_x, whole_x, whole_y, *rest = refs
    from_z = rest.pop(0) if lines else None
    local_sem, send, recv = rest
    y, x, c, z, to_x, to_y, to_p, dp = places()
    half = out_ref.shape[-2] // 2
    low, high = pl.ds(0, half), pl.ds(half, half)
    z_peers = [(dp, (z + j) % 4) for j in range(1, 4)] if lines else []
    peers = z_peers + [to_x, to_y, to_p]
    barrier = pltpu.get_barrier_semaphore()
    for peer in peers:
        hello(peer)
    pl.semaphore_wait(barrier, len(peers))
    steps = [1, 2, 3, 0] if lines else list(range(count))
    order = [(z + j) % 4 if lines else j for j in steps]
    started = []

    def go(kind, j, src, dst, peer):
        copy = remote(src, dst, send.at[kind, j], recv.at[kind, j], peer)
        copy.start()
        started.append(copy)
        return copy

    firsts, seconds, thirds, along = [], [], [], []
    for j in range(count):
        other = go(1, j, in_ref.at[:, :, 1 - c, order[j]], from_p.at[j], to_p)
        local = pltpu.make_async_copy(in_ref.at[:, :, c, order[j]], own.at[j], local_sem.at[j])
        local.start()
        firsts.append((other, local))
    for j in range(count):
        firsts[j][1].wait()
        firsts[j][0].wait_recv()
        far = own.at[j, 1 - y, 1 - x]
        add_rows(far, [far, from_p.at[j, 1 - y, 1 - x]])
        seconds.append(
            (
                go(2, j, far.at[low], from_y.at[j], to_y),
                go(3, j, far.at[high], from_x.at[j], to_x),
            )
        )
        for yy, xx in ((y, 1 - x), (1 - y, x), (y, x)):
            add_rows(own.at[j, yy, xx], [own.at[j, yy, xx], from_p.at[j, yy, xx]])
    for j in range(count):
        seconds[j][0].wait_recv()
        side = own.at[j, y, 1 - x]
        add_rows(side.at[low], [side.at[low], from_y.at[j]])
        one = go(4, j, side, whole_x.at[j], to_x)
        seconds[j][1].wait_recv()
        side = own.at[j, 1 - y, x]
        add_rows(side.at[high], [side.at[high], from_x.at[j]])
        thirds.append((one, go(5, j, side, whole_y.at[j], to_y)))
    for j in range(count):
        thirds[j][0].wait_recv()
        thirds[j][1].wait_recv()
        mine = own.at[j, y, x]
        parts = [mine, whole_x.at[j], whole_y.at[j]]
        if not lines:
            add_rows(out_ref.at[j], parts)
        elif steps[j]:
            add_rows(mine, parts)
            at = steps[j] - 1
            along.append(go(0, steps[j], mine, from_z.at[at], z_peers[at]))
        else:
            for copy in along:
                copy.wait_recv()
            add_rows(out_ref, parts + [from_z.at[k] for k in range(3)])
    for copy in started:
        copy.wait_send()


def scatter_line_body(in_ref, out_ref, own, from_low, from_high, local_sem, send, recv):
    y, x, c, z, to_x, to_y, to_p, dp = places()
    greet(True, False, z, dp, ())
    local = pltpu.make_async_copy(in_ref, own, local_sem)
    local.start()

    def up(s):
        return remote(
            own.at[s], from_low.at[s], send.at[0, s], recv.at[0, s], (dp, z + 1)
        )

    def down(s):
        return remote(
            own.at[s], from_high.at[s], send.at[1, s], recv.at[1, s], (dp, z - 1)
        )

    def take(copy, s, arrived):
        copy(s).wait_recv()
        add_rows(own.at[s], [own.at[s], arrived.at[s]])

    def rising(s):
        pl.when(z > 0)(lambda: take(up, s, from_low))
        up(s).start()

    def falling(s):
        pl.when(z < 3)(lambda: take(down, s, from_high))
        down(s).start()

    local.wait()
    order = [jnp.where(z < 2, b, 3 - b) for b in (3, 0, 2, 1)]
    for s in order:
        pl.when(z < s)(functools.partial(rising, s))
        pl.when(z > s)(functools.partial(falling, s))
    pl.when(z > 0)(lambda: take(up, z, from_low))
    pl.when(z < 3)(lambda: take(down, z, from_high))
    add_rows(out_ref, [own.at[z]])
    for s in order:
        pl.when(z < s)(lambda s=s: up(s).wait_send())
        pl.when(z > s)(lambda s=s: down(s).wait_send())


def scatter_line(parts, identity):
    return pl.pallas_call(
        scatter_line_body,
        out_shape=jax.ShapeDtypeStruct(parts.shape[1:], parts.dtype),
        in_specs=[pl.BlockSpec(memory_space=pl.ANY)],
        out_specs=pl.BlockSpec(memory_space=pltpu.VMEM),
        scratch_shapes=[
            pltpu.VMEM(parts.shape, parts.dtype),
            pltpu.VMEM(parts.shape, parts.dtype),
            pltpu.VMEM(parts.shape, parts.dtype),
            pltpu.SemaphoreType.DMA,
            pltpu.SemaphoreType.DMA((2, 4)),
            pltpu.SemaphoreType.DMA((2, 4)),
        ],
        compiler_params=pltpu.CompilerParams(
            collective_id=identity, has_side_effects=True, vmem_limit_bytes=32 * 2**20
        ),
    )(parts)


def scatter(parts, lines, identity):
    count, rows, columns = parts.shape[-3:]
    buffer = lambda *lead: pltpu.VMEM(lead + (rows, columns), parts.dtype)
    halves = pltpu.VMEM((count, rows // 2, columns), parts.dtype)
    scratch = [buffer(count, 2, 2), buffer(count, 2, 2), halves, halves, buffer(count), buffer(count)]
    if lines:
        scratch.append(buffer(3))
    scratch += [
        pltpu.SemaphoreType.DMA((count,)),
        pltpu.SemaphoreType.DMA((6, count)),
        pltpu.SemaphoreType.DMA((6, count)),
    ]
    return pl.pallas_call(
        functools.partial(scatter_body, count, lines),
        out_shape=jax.ShapeDtypeStruct(
            (rows, columns) if lines else (count, rows, columns), parts.dtype
        ),
        in_specs=[pl.BlockSpec(memory_space=pl.ANY)],
        out_specs=pl.BlockSpec(memory_space=pltpu.VMEM),
        scratch_shapes=scratch,
        compiler_params=pltpu.CompilerParams(
            collective_id=identity, has_side_effects=True, vmem_limit_bytes=48 * 2**20
        ),
    )(parts)


PIECES = 4


class Moves:
    def __init__(self, ND, NF):
        self.ND, self.NF = ND, NF
        self.fast = (ND, NF) == (8, 4)

    def gather_dp(self, rows, identity):
        if not self.fast:
            return lax.all_gather(rows, "dp", axis=0, tiled=True)
        T, C = rows.shape
        return gather(rows.reshape(PIECES, T // PIECES, C), False, True, identity).reshape(
            self.ND * T, C
        )

    def gather_fsdp(self, rows, identity):
        if not self.fast:
            return lax.all_gather(rows, "fsdp", axis=0, tiled=False)
        return gather(rows[None], True, False, identity)

    def gather_all(self, rows, identity):
        if not self.fast:
            return lax.all_gather(rows, BOTH, axis=0, tiled=False)
        return gather(rows[None], True, True, identity).reshape((-1,) + rows.shape)

    def scatter_dp(self, parts, identity):
        if not self.fast:
            return lax.psum_scatter(parts, "dp", scatter_dimension=0, tiled=True)
        T, C = parts.shape[0] // self.ND, parts.shape[1]
        return scatter(
            parts.reshape(2, 2, 2, PIECES, T // PIECES, C), False, identity
        ).reshape(T, C)

    def scatter_fsdp(self, parts, identity):
        if not self.fast:
            return lax.psum_scatter(parts, "fsdp", scatter_dimension=0, tiled=False)
        return scatter_line(parts, identity)

    def scatter_all(self, parts, identity):
        count, R, C = parts.shape
        if not self.fast:
            return lax.psum_scatter(
                parts.reshape(count * R, C), BOTH, scatter_dimension=0, tiled=True
            )
        return scatter(parts.reshape(2, 2, 2, self.NF, R, C), True, identity)


def pack(pieces):
    packed = jnp.concatenate([piece.reshape(-1, LANES) for piece in pieces], axis=0)
    return jnp.pad(packed, ((0, -packed.shape[0] % 16), (0, 0)))


def unpack(full, pieces):
    out, at = [], 0
    for piece in pieces:
        size = piece.size // LANES
        part = full[:, at : at + size]
        out.append(part.reshape(full.shape[0] * piece.shape[0], piece.shape[1]))
        at += size
    return lax.optimization_barrier(tuple(out))


def pack_grads(grads, count):
    packed = jnp.concatenate([g.astype(BF16).reshape(count, -1, LANES) for g in grads], axis=1)
    return jnp.pad(packed, ((0, 0), (0, -packed.shape[1] % 64), (0, 0)))


def unpack_grads(summed, grads, count):
    out, at = [], 0
    for g in grads:
        size = g.size // count // LANES
        out.append(summed[at : at + size].reshape(g.shape[0] // count, g.shape[1]).astype(F32))
        at += size
    return out


def per_device_of(ND, NF):
    COUNT = ND * NF
    moves = Moves(ND, NF)

    def per_device(
        layer_input,
        output_gradient,
        prefix_length,
        attention_gain,
        inward,
        inward_down,
        inward_up,
        outward,
        outward_down,
        outward_up,
        feedforward_gain,
        widening,
        widening_down,
        widening_up,
        narrowing,
        narrowing_down,
        narrowing_up,
    ):
        micro_count, _, T, D = layer_input.shape
        QKV = inward.shape[1]
        query_width = outward.shape[0] * COUNT
        HEADS = query_width // HDIM
        FF = widening.shape[1] // 2
        RANK = widening_down.shape[1]
        FS = FF // ND
        FP = -(-FS // LANES) * LANES
        ROWS = D // COUNT
        UPS = RANK // COUNT
        scale = HDIM ** (-0.5)

        gains = jnp.pad(
            jnp.stack([attention_gain, feedforward_gain]), ((0, 0), (0, LANES - ROWS))
        )
        pieces = (
            gains,
            inward,
            inward_down,
            inward_up,
            outward,
            outward_down,
            outward_up,
            widening_down,
            narrowing_up,
        )
        (
            gains_full,
            inward_full,
            inward_down_full,
            inward_up_full,
            outward_full,
            outward_down_full,
            outward_up_full,
            widening_down_full,
            narrowing_up_full,
        ) = unpack(moves.gather_all(pack(pieces), 1), pieces)
        gains_full = gains_full.reshape(COUNT, 2, LANES)[:, :, :ROWS].astype(F32)
        first_gain = gains_full[:, 0].reshape(D)
        second_gain = gains_full[:, 1].reshape(D)
        wide = jnp.concatenate([widening, widening_up], axis=0)
        wide = wide.reshape(ROWS + UPS, 2, ND, FS)
        wide = jnp.pad(wide, ((0, 0), (0, 0), (0, 0), (0, FP - FS)))
        wide = wide.transpose(2, 0, 1, 3).reshape(ND, ROWS + UPS, 2 * FP)
        wide = lax.all_to_all(wide, "dp", 0, 0, tiled=True)
        wide = lax.all_gather(wide, "fsdp", axis=0, tiled=False)
        wide = wide.transpose(1, 0, 2, 3)
        widening_slice = wide[:, :, :ROWS].reshape(D, 2 * FP)
        widening_up_slice = wide[:, :, ROWS:].reshape(RANK, 2 * FP)
        narrow = jnp.concatenate([narrowing, narrowing_down], axis=1)
        narrow = lax.all_gather(narrow, "fsdp", axis=0, tiled=True)
        narrow = jnp.pad(narrow, ((0, FP - FS), (0, 0)))
        narrowing_slice, narrowing_down_slice = narrow[:, :D], narrow[:, D:]

        inward_eff = (inward_full + product(inward_down_full, inward_up_full)).astype(BF16)
        outward_eff = (outward_full + product(outward_down_full, outward_up_full)).astype(BF16)
        wide_eff = (widening_slice + product(widening_down_full, widening_up_slice)).astype(BF16)
        narrow_eff = (narrowing_slice + product(narrowing_down_slice, narrowing_up_full)).astype(
            BF16
        )

        positions = lax.axis_index("fsdp") * T + jnp.arange(T, dtype=jnp.int32)
        cosine, sine_part = rotation(positions, HDIM)

        def unit(v):
            return v * lax.rsqrt(jnp.mean(v * v, axis=-1, keepdims=True) + EPSILON)

        def unit_back(v, gain, upstream):
            r = lax.rsqrt(jnp.mean(v * v, axis=-1, keepdims=True) + EPSILON)
            n = v * r
            e = upstream * gain
            back = r * (e - n * jnp.mean(e * n, axis=-1, keepdims=True))
            return back, jnp.sum(upstream * n, axis=0)

        M = micro_count
        R = M * T
        per_micro = lambda a: a.reshape((M, T) + a.shape[1:])
        cosine_all = jnp.concatenate([cosine] * M, axis=0)
        sine_all = jnp.concatenate([sine_part] * M, axis=0)
        head_cosine, head_sine = cosine_all[:, None, :], sine_all[:, None, :]

        residual = layer_input.reshape(R, D).astype(F32)
        upstream = output_gradient.reshape(R, D)
        upstream_all = lax.all_gather(upstream, "dp", axis=0, tiled=True)

        normed_first = (unit(residual) * first_gain).astype(BF16)
        joint = product(normed_first, inward_eff)
        queries = rotate(
            joint[:, :query_width].reshape(R, HEADS, HDIM), head_cosine, head_sine
        ).astype(BF16)
        queries = per_micro(queries)
        own_keys = rotate(joint[:, query_width : query_width + HDIM], cosine_all, sine_all)
        own = jnp.concatenate([own_keys, joint[:, query_width + HDIM :]], axis=1).astype(BF16)
        both = moves.gather_fsdp(own, 3).reshape(NF, M, T, 2 * HDIM)
        both = both.transpose(1, 0, 2, 3).reshape(M, NF * T, 2 * HDIM)
        all_keys, all_values = both[..., :HDIM], both[..., HDIM:]
        key_pos = jnp.arange(NF * T, dtype=jnp.int32)
        visible = (key_pos[None, None, :] <= positions[None, :, None]) | (
            key_pos[None, None, :] < prefix_length[:, :, None]
        )

        def masked_scores():
            raw = (
                jnp.einsum("mrhd,mkd->mhrk", queries, all_keys, preferred_element_type=F32) * scale
            )
            return jnp.where(visible[:, None], raw, -1e30)

        scores = masked_scores()
        peak = jnp.max(scores, axis=-1, keepdims=True)
        logsum = peak + jnp.log(jnp.sum(jnp.exp(scores - peak), axis=-1, keepdims=True))
        probs_low = jnp.exp(scores - logsum).astype(BF16)
        mix = jnp.einsum("mhrk,mkd->mrhd", probs_low, all_values, preferred_element_type=F32)
        mixed = mix.reshape(R, query_width).astype(BF16)
        middle = residual + product(mixed, outward_eff)
        normed_second = (unit(middle) * second_gain).astype(BF16)
        second_all = moves.gather_dp(normed_second, 4)

        spread = product(second_all, wide_eff)
        gate, upper = spread[:, :FP], spread[:, FP:]
        value, slope = gelu_parts(gate)
        activated = (value * upper).astype(BF16)
        shrink = product(activated, narrow_eff).astype(BF16)
        shrink = lax.psum_scatter(shrink, "dp", scatter_dimension=0, tiled=True)
        outputs = (middle + shrink.astype(F32)).astype(BF16)
        narrow_grad = contract_rows(activated, upstream_all).astype(BF16)
        act_grad = against(upstream_all, narrow_eff)
        spread_grad = jnp.concatenate(
            [act_grad * upper * slope, act_grad * value], axis=1
        ).astype(BF16)
        wide_grad = contract_rows(second_all, spread_grad).astype(BF16)
        rows_grad = against(spread_grad, wide_eff).astype(BF16)
        rows_grad = moves.scatter_dp(rows_grad, 5)
        back, second_gain_grad = unit_back(middle, second_gain, rows_grad.astype(F32))
        middle_grad = upstream.astype(F32) + back
        branch_grad = middle_grad.astype(BF16)

        wide_up_grad = contract_rows(widening_down_full, wide_grad).astype(BF16)
        widening_down_part = against(wide_grad, widening_up_slice)
        narrowing_up_part = contract_rows(narrowing_down_slice, narrow_grad)
        wide_both = jnp.concatenate(
            [
                wide_grad.reshape(ND, NF, ROWS, 2 * FP),
                wide_up_grad.reshape(ND, NF, UPS, 2 * FP),
            ],
            axis=2,
        ).transpose(1, 0, 2, 3)
        wide_both = wide_both.reshape(NF * ND * (ROWS + UPS), 2 * FP)
        wide_both = lax.psum_scatter(wide_both, "fsdp", scatter_dimension=0, tiled=True)
        wide_both = wide_both.reshape(ND, ROWS + UPS, 2 * FP)
        wide_both = lax.all_to_all(wide_both, "dp", 0, 0, tiled=True)
        wide_both = wide_both.reshape(ND, ROWS + UPS, 2, FP)[..., :FS].transpose(1, 2, 0, 3)
        wide_both = wide_both.reshape(ROWS + UPS, 2 * FF).astype(F32)
        widening_grad, widening_up_grad = wide_both[:ROWS], wide_both[ROWS:]
        narrow_sum = lax.psum_scatter(narrow_grad[:FS], "fsdp", scatter_dimension=0, tiled=True)
        narrowing_grad = narrow_sum.astype(F32)
        narrowing_down_grad = against(narrow_sum, narrowing_up_full)

        mixed_grad = against(branch_grad, outward_eff).astype(BF16)
        mixed_grad = mixed_grad.reshape(M, T, HEADS, HDIM)
        probs_again = jnp.exp(masked_scores() - logsum)
        prob_grad = jnp.einsum(
            "mrhd,mkd->mhrk", mixed_grad, all_values, preferred_element_type=F32
        )
        center = jnp.sum(probs_again * prob_grad, axis=-1, keepdims=True)
        score_grad = (probs_again * (prob_grad - center)).astype(BF16)
        key_grad = (
            jnp.einsum("mhrk,mrhd->mkd", score_grad, queries, preferred_element_type=F32) * scale
        )
        value_grad = jnp.einsum(
            "mhrk,mrhd->mkd", probs_again.astype(BF16), mixed_grad, preferred_element_type=F32
        )
        both = jnp.concatenate([key_grad, value_grad], axis=-1).astype(BF16)
        both = both.reshape(M, NF, T, 2 * HDIM).transpose(1, 0, 2, 3).reshape(NF, R, 2 * HDIM)
        both = moves.scatter_fsdp(both, 7).astype(F32)
        query_grad = (
            jnp.einsum("mhrk,mkd->mrhd", score_grad, all_keys, preferred_element_type=F32) * scale
        ).reshape(R, HEADS, HDIM)
        joint_grad = jnp.concatenate(
            [
                rotate(query_grad, head_cosine, -head_sine).reshape(R, query_width),
                rotate(both[:, :HDIM], cosine_all, -sine_all),
                both[:, HDIM:],
            ],
            axis=1,
        ).astype(BF16)
        first_rows_grad = against(joint_grad, inward_eff)
        back, first_gain_grad = unit_back(residual, first_gain, first_rows_grad)
        input_grads = middle_grad + back

        outward_part = contract_rows(mixed, branch_grad).astype(BF16)
        outward_up_part = contract_rows(outward_down_full, outward_part)
        inward_part = contract_rows(normed_first, joint_grad).astype(BF16)
        inward_up_part = contract_rows(inward_down_full, inward_part)
        gain_parts = jnp.stack([first_gain_grad, second_gain_grad]).reshape(2, COUNT, ROWS)
        gain_parts = jnp.pad(gain_parts, ((0, 0), (0, 0), (0, LANES - ROWS)))
        gain_parts = gain_parts.transpose(1, 0, 2).reshape(COUNT * 2, LANES)
        parts = (
            outward_part,
            outward_up_part,
            widening_down_part,
            narrowing_up_part,
            inward_part,
            inward_up_part,
            gain_parts,
        )
        (
            outward_grad,
            outward_up_grad,
            widening_down_grad,
            narrowing_up_grad,
            inward_grad,
            inward_up_grad,
            gain_grads,
        ) = unpack_grads(moves.scatter_all(pack_grads(parts, COUNT), 6), parts, COUNT)
        outward_down_grad = against(outward_grad.astype(BF16), outward_up_full)
        inward_down_grad = against(inward_grad.astype(BF16), inward_up_full)

        return (
            outputs.reshape(layer_input.shape),
            input_grads.reshape(layer_input.shape),
            gain_grads[0, :ROWS],
            inward_grad,
            inward_down_grad,
            inward_up_grad,
            outward_grad,
            outward_down_grad,
            outward_up_grad,
            gain_grads[1, :ROWS],
            widening_grad,
            widening_down_grad,
            widening_up_grad,
            narrowing_grad,
            narrowing_down_grad,
            narrowing_up_grad,
        )

    return per_device


def solution(mesh):
    rows = P(BOTH, None)
    tokens = P(None, "dp", "fsdp", None)
    weights = (P(BOTH),) + (rows,) * 6 + (P(BOTH),) + (rows,) * 6
    return jax.shard_map(
        per_device_of(mesh.shape["dp"], mesh.shape["fsdp"]),
        mesh=mesh,
        in_specs=(tokens, tokens, P(None, "dp")) + weights,
        out_specs=(tokens, tokens) + weights,
        check_vma=False,
    )
```

time: 1270 us -> 840 us (0.66)
  waiting for transfers between devices: 746 us -> 66.3 us
  Pallas kernels: 0 us -> 290 us
  matrix products: 241 us -> 198 us
  local copies, waits for them, and re-layouts: 149 us -> 190 us
  other arithmetic: 74.6 us -> 39.2 us
    reduce_scatter x6 -> x0, waiting for transfers between devices: 316 us -> none  [the longest x2 224 us: scatter_packed(): lax.psum_scatter(packed.reshape(count * rows, LANES), BOTH, scatter_dimen...]
    pallas_call x0 -> x6, Pallas kernels: none -> 290 us  [the longest x3 148 us: gather(): pl.pallas_call(functools.partial(gather_body, count, lines, planes), out_...]
    all_gather x8 -> x1, waiting for transfers between devices: 178 us -> 0.01 us  [per_device(): upstream_all = lax.all_gather(upstream, 'dp', axis=0, tiled=True)]
    all_gather x1, waiting for transfers between devices: 81.3 us -> 0.01 us  [per_device(): wide = lax.all_gather(wide, 'fsdp', axis=0, tiled=False)]
    reduce_scatter x1, waiting for transfers between devices: 72.2 us -> 29 us  [per_device(): lax.psum_scatter(wide_both, 'fsdp', scatter_dimension=0, tiled=True)]
    all_gather x1, waiting for transfers between devices: 26.4 us -> 0.02 us  [per_device(): narrow = lax.all_gather(narrow, 'fsdp', axis=0, tiled=True)]
    reduce_scatter x2 -> x1, waiting for transfers between devices: 54.6 us -> 36.5 us  [per_device(): shrink = lax.psum_scatter(shrink, 'dp', scatter_dimension=0, tiled=True)]
    convert_element_type x13 -> x9, other arithmetic: 20.9 us -> 3.16 us  [the longest x5 1.4 us: unpack_grads(): summed[at:at + size].reshape(g.shape[0] // count, g.shape[1]).astype(F32)]
  transfers between devices with their start and end apart: 21 -> 7, of which waited for: 15 -> 2; matrix products, arithmetic and copies ran while one was open for 31% -> 29% of each run, Pallas kernels for 0% -> 24%
where the time goes in v2:
time: 840 us; the launch traced here: 828 us
  Pallas kernels  290 us (35%)
  matrix products  198 us (24%)
  local copies, waits for them, and re-layouts  190 us (23%)
  waiting for transfers between devices  66.3 us (8%)
  other arithmetic  39.2 us (5%)
  blocking collectives  23.8 us (3%)
  between operations  15.8 us (2%)
    pallas_call x3, Pallas kernels, gather(): pl.pallas_call(functools.partial(gather_body, count, lines, planes), out_...  148 us
    pallas_call x2, Pallas kernels, scatter(): pl.pallas_call(functools.partial(scatter_body, count, lines), out_shape=j...  104 us
    dot_general x8, matrix products, against(): lax.dot_general(left, right, (((1,), (1,)), ((), ())), preferred_element_...  69.9 us
    dot_general x8, matrix products, product(): return jnp.dot(left, right, preferred_element_type=F32)  56.1 us
    dot_general x8, matrix products, contract_rows(): lax.dot_general(left, right, (((0,), (0,)), ((), ())), preferred_element_...  51.9 us
    pallas_call x1, Pallas kernels, scatter_line(): pl.pallas_call(scatter_line_body, out_shape=jax.ShapeDtypeStruct(parts.sh...  37.5 us
    reduce_scatter x1, waiting for transfers between devices, per_device(): shrink = lax.psum_scatter(shrink, 'dp', scatter_dimension=0, tiled=True)  36.5 us
    unnamed x168, local copies, waits for them, and re-layouts  29.6 us
  transfers between devices with their start and end apart: 7, of which 2 were waited for; matrix products, arithmetic and copies ran while one was open for 29% of the time, Pallas kernels for 24%

profile of v2, /device:TPU:0, one launch (start us, length us, event | category | flops | bytes accessed | tf_op | source)
XLA Modules:
  0.0 827.8 jit_solution(7633802901940844658)
XLA Ops:
  15.9 23.8 %all_to_all.10 = bf16[8,44,1792]{2,1,0:T(8,128)(2,1)S(1)} all-to-all(bf16[8,44,1792]{2,1,0:T(8,128)(2,1)S(1)} %copy.101), channel_id=1, replica_groups=mesh['dp'=8,'fsdp'=4] {'dp'}, dimensions={0} | all-to-all | bytes 2523136 | tf_op jit(solution)/shard_map/all_to_all | solution.py:531
  45.3 62.5 %shard_map.288 = bf16[2,2,2,4,1184,128]{5,4,3,2,1,0:T(8,128)(2,1)} custom-call(bf16[1,1184,128]{2,1,0:T(8,128)(2,1)} %pad_bitcast_fusion.1.in_ref), custom_call_target="tpu_custom_call" | custom-call | tf_op jit(solution)/shard_map/pallas_call | solution.py:201
  112.9 3.9 slice.196
  127.1 5.7 reshape.422
  132.8 5.2 reshape.419
  138.0 3.8 fusion.57
  168.3 40.6 %shard_map.289 = bf16[4,512,512]{2,1,0:T(8,128)(2,1)} custom-call(bf16[1,512,512]{2,1,0:T(8,128)(2,1)} %pad_maximum_fusion.11.in_ref), custom_call_target="tpu_custom_call" | custom-call | tf_op jit(solution)/shard_map/pallas_call | solution.py:201
  220.7 10.7 %copy.99 = bf16[2,256,4,256]{3,2,1,0:T(4,128)(2,1)} copy(bf16[2,256,4,256]{1,3,2,0:T(8,128)(2,1)} %fusion.27) | data formatting | bytes 2097152 | tf_op jit(solution)/shard_map/convert_element_type | solution.py:599
  238.9 45.3 %shard_map.290 = bf16[2,2,2,4,128,1152]{5,4,3,2,1,0:T(8,128)(2,1)} custom-call(bf16[4,128,1152]{2,1,0:T(8,128)(2,1)} %bitcast.214), custom_call_target="tpu_custom_call" | custom-call | tf_op jit(solution)/shard_map/pallas_call | solution.py:201
  293.4 8.4 %copy.103 = f32[8,4,36,1792]{3,2,1,0:T(8,128)} copy(f32[8,4,36,1792]{3,0,1,2:T(8,128)S(1)} %slice_convert_fusion) | data formatting | bytes 16515072 | tf_op jit(solution)/shard_map/convert_element_type | solution.py:543
  301.8 9.3 %reshape.459 = f32[1152,1792]{1,0:T(8,128)} reshape(f32[8,4,36,1792]{3,2,1,0:T(8,128)} %copy.103) | data formatting | bytes 16515072 | tf_op jit(solution)/shard_map/convert_element_type | solution.py:543
  311.1 4.6 fusion.15
  317.8 25.2 %fusion.60 = f32[4096,1792]{0,1:T(8,128)} fusion(bf16[4096,1152]{1,0:T(8,128)(2,1)} %bitcast.202, bf16[1152,1792]{1,0:T(8,128)(2,1)S(1)} %fusion.15), kind=kOutput, calls=%fused_computation.159 | convolution fusion | flops 16911433728 | bytes 42926080 | tf_op jit(solution)/shard_map/dot_general | solution.py:20
  343.0 27.0 %fusion.7 = (bf16[4096,896]{0,1:T(8,128)(2,1)S(1)}, bf16[4096,896]{0,1:T(8,128)(2,1)}, bf16[4096,896]{0,1:T(8,128)(2,1)}) fusion(f32[4096,1792]{0,1:T(8,128)} %fusion.60, bf16[896,1152]{1,0:T(8,128)(2,1)} %fusion.19, bf16[4096,1152]{1,0:T(8,128)(2,1)} %all-gather.7.cloned.1.call-done), kind=kOutput, calls=%fused_computation.11 | convolution fusion | flops 8547467264 | bytes 62881792 | tf_op jit(solution)/shard_map/dot_general | solution.py:28
  369.9 26.2 %fusion.13 = bf16[1152,1792]{1,0:T(8,128)(2,1)S(1)} fusion(bf16[4096,1152]{1,0:T(8,128)(2,1)} %bitcast.203, bf16[4096,896]{0,1:T(8,128)(2,1)} %get-tuple-element.105, bf16[4096,896]{0,1:T(8,128)(2,1)S(1)} %get-tuple-element.104), kind=kOutput, calls=%fused_computation.29 | convolution fusion | flops 16942858240 | bytes 28246016 | tf_op jit(solution)/shard_map/dot_general | solution.py:24
  399.6 6.9 reshape.453
  412.2 7.4 reshape.455
  419.8 15.1 %convolution_convert_fusion.4 = bf16[896,1152]{1,0:T(8,128)(2,1)S(1)} fusion(bf16[4096,896]{0,1:T(8,128)(2,1)} %get-tuple-element.106, bf16[4096,1152]{1,0:T(8,128)(2,1)} %all-gather.7.cloned.1.call-done), kind=kOutput, calls=%fused_computation.41 | convolution fusion | flops 8456749056 | bytes 18841600 | tf_op jit(solution)/shard_map/dot_general | solution.py:24
  438.5 15.3 %convolution_convert_fusion.1 = bf16[4096,1152]{1,0:T(8,128)(2,1)} fusion(bf16[4096,896]{0,1:T(8,128)(2,1)} %get-tuple-element.106, bf16[896,1152]{1,0:T(8,128)(2,1)S(1)} %copy-done.37), kind=kOutput, calls=%fused_computation.3 | convolution fusion | flops 8460435456 | bytes 18841600 | tf_op jit(solution)/shard_map/dot_general | solution.py:20
  453.9 25.8 %convolution_convert_fusion = bf16[4096,1152]{1,0:T(8,128)(2,1)} fusion(bf16[1152,1792]{1,0:T(8,128)(2,1)} %copy-done.24, bf16[4096,896]{0,1:T(8,128)(2,1)} %get-tuple-element.105, bf16[4096,896]{0,1:T(8,128)(2,1)} %copy-done.77), kind=kOutput, calls=%fused_computation.2 | convolution fusion | flops 16945512448 | bytes 28246016 | tf_op jit(solution)/shard_map/dot_general | solution.py:28
  479.7 29.0 %reduce-scatter.8.cloned.1.call-done = bf16[352,1792]{1,0:T(8,128)(2,1)} async-done(((bf16[1408,1792]{1,0:T(8,128)(2,1)}), bf16[352,1792]{1,0:T(8,128)(2,1)}) %reduce-scatter.8.cloned.1.call-update) | async-done | bytes 1261584 | tf_op jit(solution)/shard_map/reduce_scatter | solution.py:634
  511.0 4.5 all-to-all-start.1
  520.1 51.8 %shard_map.291 = bf16[4,128,1152]{2,1,0:T(8,128)(2,1)S(1)} custom-call(bf16[2,2,2,4,128,1152]{5,4,3,2,1,0:T(8,128)(2,1)} %bitcast.204), custom_call_target="tpu_custom_call" | custom-call | tf_op jit(solution)/shard_map/pallas_call | solution.py:373
  596.6 36.5 %reduce-scatter.6.cloned.1.call-done = bf16[512,1152]{1,0:T(8,128)(2,1)} async-done(((bf16[4096,1152]{1,0:T(8,128)(2,1)}), bf16[512,1152]{1,0:T(8,128)(2,1)}) %reduce-scatter.6.cloned.1.call-update) | async-done | bytes 1179664 | tf_op jit(solution)/shard_map/reduce_scatter | solution.py:609
  648.1 5.7 bitcast_convert_fusion
  653.9 5.9 fusion.10
  665.6 37.5 %shard_map.292 = bf16[512,512]{1,0:T(8,128)(2,1)S(1)} custom-call(bf16[4,512,512]{2,1,0:T(8,128)(2,1)S(1)} %bitcast.191), custom_call_target="tpu_custom_call" | custom-call | tf_op jit(solution)/shard_map/pallas_call | solution.py:342
  709.5 6.8 multiply_reduce_fusion
  722.3 6.4 reshape.448
  749.3 8.0 pad.30
  757.3 52.3 %shard_map.293 = bf16[1088,128]{1,0:T(8,128)(2,1)S(1)} custom-call(bf16[2,2,2,4,1088,128]{5,4,3,2,1,0:T(8,128)(2,1)} %bitcast.200), custom_call_target="tpu_custom_call" | custom-call | tf_op jit(solution)/shard_map/pallas_call | solution.py:373
  816.3 4.4 multiply_add_fusion.1
  (317 shorter events, 190.3 us)
Async XLA Ops:
  7.2 277.1 %all-gather.5.cloned.1.call-start = ((), (), s32[]{:S(2)}) async-start(), calls=%async_computation.5 | async-start | bytes 3041280 | tf_op jit(solution)/shard_map/all_gather | solution.py:537
  9.2 278.9 %all-gather.9.cloned.1.call-start = ((), (), s32[]{:S(2)}) async-start(), calls=%async_computation.9 | async-start | bytes 6307840 | tf_op jit(solution)/shard_map/all_gather | solution.py:532
  41.2 301.8 %all-gather.7.cloned.1.call-start = ((), (), s32[]{:S(2)}) async-start(), calls=%async_computation.7 | async-start | bytes 10616832 | tf_op jit(solution)/shard_map/all_gather | solution.py:570
  42.0 466.7 %reduce-scatter.8.cloned.1.call-start = ((), (), s32[]{:S(2)}) async-start(), calls=%async_computation.8 | async-start | bytes 6307840 | tf_op jit(solution)/shard_map/reduce_scatter | solution.py:634
  141.8 11.6 %copy-start.4 = (bf16[1152,1536]{1,0:T(8,128)(2,1)S(1)}, bf16[1152,1536]{1,0:T(8,128)(2,1)}, u32[]{:S(2)}) copy-start(bf16[1152,1536]{1,0:T(8,128)(2,1)} %reshape.419) | copy-start | bytes 10616836
  152.6 83.6 %copy-start.52 = (f32[1152]{0:T(1024)}, f32[1152]{0:T(1024)S(1)}, u32[]{:S(2)}) copy-start(f32[1152]{0:T(1024)S(1)} %mul.316) | copy-start | bytes 13828
  166.3 45.6 %copy-start.31 = (f32[512,128]{1,0:T(8,128)}, f32[512,128]{1,0:T(8,128)S(1)}, u32[]{:S(2)}) copy-start(f32[512,128]{1,0:T(8,128)S(1)} %get-tuple-element.127) | copy-start | bytes 786436
  168.3 42.5 %copy-start.74 = (s32[2,1]{0,1:T(1,128)S(1)}, s32[2,1]{0,1:T(1,128)}, u32[]{:S(2)}) copy-start(s32[2,1]{0,1:T(1,128)} %param.19) | copy-start | bytes 28
  220.7 12.2 %copy-start.10 = (bf16[1024,1152]{1,0:T(8,128)(2,1)S(1)}, bf16[1024,1152]{1,0:T(8,128)(2,1)}, u32[]{:S(2)}) copy-start(bf16[1024,1152]{1,0:T(8,128)(2,1)} %reshape.422) | copy-start | bytes 7077892
  220.7 12.2 %copy-start.19 = (bf16[256,1152]{1,0:T(8,128)(2,1)S(1)}, bf16[256,1152]{1,0:T(8,128)(2,1)}, u32[]{:S(2)}) copy-start(bf16[256,1152]{1,0:T(8,128)(2,1)} %reshape.424) | copy-start | bytes 1769476
  220.7 12.2 %copy-start.21 = (bf16[1024,256]{1,0:T(8,128)(2,1)S(1)}, bf16[1024,256]{1,0:T(8,128)(2,1)}, u32[]{:S(2)}) copy-start(bf16[1024,256]{1,0:T(8,128)(2,1)} %reshape.423) | copy-start | bytes 1572868
  238.9 45.4 %copy-start.18 = (bf16[256,1152]{1,0:T(8,128)(2,1)S(1)}, bf16[256,1152]{1,0:T(8,128)(2,1)}, u32[]{:S(2)}) copy-start(bf16[256,1152]{1,0:T(8,128)(2,1)} %reshape.426) | copy-start | bytes 1769476
  289.8 21.2 %copy-start.25 = (bf16[8,4,8,1792]{3,2,1,0:T(8,128)(2,1)}, bf16[8,4,8,1792]{3,2,1,0:T(8,128)(2,1)S(1)}, u32[]{:S(2)}) copy-start(bf16[8,4,8,1792]{3,2,1,0:T(8,128)(2,1)S(1)} %copy.104) | copy-start | bytes 2752516
  301.8 9.3 %copy-start.36 = (bf16[1152,256]{1,0:T(8,128)(2,1)S(1)}, bf16[1152,256]{1,0:T(8,128)(2,1)}, u32[]{:S(2)}) copy-start(bf16[1152,256]{1,0:T(8,128)(2,1)} %reshape.425) | copy-start | bytes 1769476
  369.9 26.2 %copy-start.77 = (bf16[4096,896]{0,1:T(8,128)(2,1)}, bf16[4096,896]{0,1:T(8,128)(2,1)S(1)}, u32[]{:S(2)}) copy-start(bf16[4096,896]{0,1:T(8,128)(2,1)S(1)} %get-tuple-element.104) | copy-start | bytes 22020100
  419.7 159.2 %reduce-scatter.10.cloned.1.call-start = ((), (), s32[]{:S(2)}) async-start(), calls=%async_computation.10 | async-start | bytes 2488320
  437.7 195.4 %reduce-scatter.6.cloned.1.call-start = ((), (), s32[]{:S(2)}) async-start(), calls=%async_computation.6 | async-start | bytes 10616832 | tf_op jit(solution)/shard_map/reduce_scatter | solution.py:609
  479.7 35.8 %copy-start.26 = (bf16[8,4,8,1792]{3,2,1,0:T(8,128)(2,1)S(1)}, bf16[8,4,8,1792]{3,2,1,0:T(8,128)(2,1)}, u32[]{:S(2)}) copy-start(bf16[8,4,8,1792]{3,2,1,0:T(8,128)(2,1)} %copy-done.25) | copy-start | bytes 2752516
  511.0 72.3 %all-to-all-start.1 = ((bf16[8,44,1792]{2,1,0:T(8,128)(2,1)}), bf16[8,44,1792]{2,1,0:T(8,128)(2,1)}, u32[]{:S(2)}, u32[]{:S(2)}) async-start(bf16[8,44,1792]{2,1,0:T(8,128)(2,1)} %reshape.456), calls=%async_computation.3 | async-start | bytes 2752512 | tf_op jit(solution)/shard_map/all_to_all | solution.py:636
  520.1 51.8 %copy-start.1 = (bf16[864,1408]{1,0:T(8,128)(2,1)S(1)}, bf16[864,1408]{1,0:T(8,128)(2,1)}, u32[]{:S(2)}) copy-start(bf16[864,1408]{1,0:T(8,128)(2,1)} %all-gather.5.cloned.1.call-done) | copy-start | bytes 7299076
  520.1 51.8 %copy-start.16 = (bf16[896,1152]{1,0:T(8,128)(2,1)S(1)}, bf16[896,1152]{1,0:T(8,128)(2,1)}, u32[]{:S(2)}) copy-start(bf16[896,1152]{1,0:T(8,128)(2,1)} %copy-done.15) | copy-start | bytes 6193156
  648.1 5.8 copy-start.14
  648.1 11.7 %slice-start = ((s8[8388608]{0:T(1024)(128)(4,1)}), s8[4194304]{0:T(1024)(128)(4,1)S(1)}, s32[]{:S(2)}) async-start(s8[8388608]{0:T(1024)(128)(4,1)} %bitcast.192), calls=%async_computation.11 | async-start | bytes 8388608
  653.9 5.9 slice-start.1
  709.5 6.8 copy-start.42
  709.5 6.8 copy-start.51
  734.7 10.4 %copy-start.62 = (bf16[1,32,36]{2,1,0:T(8,128)(2,1)S(1)}, bf16[1,32,36]{2,1,0:T(8,128)(2,1)}, u32[]{:S(2)}) copy-start(bf16[1,32,36]{2,1,0:T(8,128)(2,1)} %stack.22) | copy-start | bytes 6916
  739.1 6.1 copy-start.63
  757.3 52.5 %copy-start.20 = (bf16[256,1152]{1,0:T(8,128)(2,1)S(1)}, bf16[256,1152]{1,0:T(8,128)(2,1)}, u32[]{:S(2)}) copy-start(bf16[256,1152]{1,0:T(8,128)(2,1)} %reshape.424) | copy-start | bytes 1769476
  757.3 54.3 %copy-start.17 = (bf16[256,1536]{1,0:T(8,128)(2,1)S(1)}, bf16[256,1536]{1,0:T(8,128)(2,1)}, u32[]{:S(2)}) copy-start(bf16[256,1536]{1,0:T(8,128)(2,1)} %reshape.421) | copy-start | bytes 2359300
  809.6 6.7 copy-start.8
  809.7 6.7 copy-start.71
  (55 other events, 140.9 us)
Sparse Core Ops, SparseCore 0:
  9.6 60.4 all-gather.4
  71.7 95.1 all-gather.8
  168.7 56.5 all-gather.6
  419.8 88.8 reduce-scatter.7
  510.8 42.4 reduce-scatter.9
  556.7 76.3 reduce-scatter.5
